TPU v7x, 512 devices: a whole 4x8x8 slice. The times are simulated.
512 devices in a mesh: batch: 4 (over x_hi, core), space: 128 (over x_lo, y, z).
Axes of the slice: x: 4 (x_hi: 2, x_lo: 2; x = x_hi * 2 + x_lo), y: 8, z: 8, core: 2. Of those that a mesh axis runs over, the one named last changes fastest.
Arguments:
- inputs: bfloat16 [4, 32, 128, 128, 128], P('batch', None, None, 'space'), may hold values from -6 to 6
- pre_act: bfloat16 [4, 32, 128, 128, 128], P('batch', None, None, 'space'), may hold values from -8 to 8
- cotangent: bfloat16 [4, 32, 128, 128, 128], P('batch', None, None, 'space'), may hold values from -6 to 6
- spectral_weight: bfloat16 [2, 32, 32, 16384], P(None, None, None, 'space'), may hold values from -6 to 6
- skip_weight: bfloat16 [32, 32], replicated, may hold values from -1 to 1
Outputs:
- grad_inputs: bfloat16 [4, 32, 128, 128, 128], P('batch', None, None, 'space')
- grad_spectral: float32 [2, 32, 32, 16384], P(None, None, 'batch', 'space')
- grad_skip: float32 [32, 32], replicated
All inputs are finite; a program needn't handle non-finite values.
Results may differ from a plain program's by a relative error of at most 0.0055.
Values sent between devices are 32-bit elements; how exact they have to be, the bound alone decides.
A program may use at most 64 MiB of HBM per device.

v0:
```python
import math

import jax
import jax.numpy as jnp
from jax import lax
from jax.sharding import PartitionSpec as P

NX = 128
NY = 128
NZ = 128
MX = 16
MY = 16
MZ = 16


HIGHEST = lax.Precision.HIGHEST


def phase_table(length, count, signed):
    points = jnp.arange(length, dtype=jnp.int32)
    orders = jnp.arange(count, dtype=jnp.int32)
    if signed:
        orders = jnp.where(orders < count // 2, orders, orders - count)
    residues = jnp.mod(points[:, None] * orders[None, :], length)
    radians = residues.astype(jnp.float32) * (2.0 * math.pi / length)
    return (jnp.cos(radians), jnp.sin(radians))


def forward_block(cosine, sine):
    return jnp.stack(
        [jnp.stack([cosine, -sine], axis=1), jnp.stack([sine, cosine], axis=1)], axis=0
    )


def inverse_block(cosine, sine):
    cos_rows = cosine.T
    sin_rows = sine.T
    return jnp.stack(
        [jnp.stack([cos_rows, sin_rows], axis=1), jnp.stack([-sin_rows, cos_rows], axis=1)], axis=0
    )


def gelu_slope(values):
    normal_cdf = 0.5 * (1.0 + jax.scipy.special.erf(values * (1.0 / math.sqrt(2.0))))
    density = jnp.exp(-0.5 * values * values) * (1.0 / math.sqrt(2.0 * math.pi))
    return normal_cdf + values * density


def local_spectrum(grid_in):
    cos_x, sin_x = phase_table(NX, 2 * MX, True)
    table_x = jnp.stack([cos_x, -sin_x], axis=1).astype(jnp.bfloat16)
    section_x = jnp.einsum(
        "scxyz,xpa->scpayz", grid_in, table_x, preferred_element_type=jnp.float32
    )
    cos_z, sin_z = phase_table(NZ, MZ, False)
    section_z = jnp.einsum(
        "scpayz,pzqk->scqyak", section_x, forward_block(cos_z, sin_z), precision=HIGHEST
    )
    return section_z.reshape(
        section_z.shape[0], section_z.shape[1], 2, section_z.shape[3], 2 * MX * MZ
    )


def along_y(spectra):
    cos_y, sin_y = phase_table(NY, 2 * MY, True)
    section_y = jnp.einsum(
        "scpym,pyqk->scqmk", spectra, forward_block(cos_y, sin_y), precision=HIGHEST
    )
    return section_y.reshape(section_y.shape[0], section_y.shape[1], 2, section_y.shape[3] * 2 * MY)


def both_along_y(spectra_pair):
    return (along_y(spectra_pair[0]), along_y(spectra_pair[1]))


def to_grid(spectra):
    shaped = spectra.reshape(spectra.shape[0], spectra.shape[1], 2, spectra.shape[3], 2 * MX, MZ)
    cos_z, sin_z = phase_table(NZ, MZ, False)
    grid_z = jnp.einsum(
        "scpyak,pkqz->scqayz", shaped, inverse_block(cos_z, sin_z), precision=HIGHEST
    )
    cos_x, sin_x = phase_table(NX, 2 * MX, True)
    table_x = jnp.stack([cos_x.T, -sin_x.T], axis=0)
    return jnp.einsum("scpayz,pax->scxyz", grid_z, table_x, precision=HIGHEST)


def cross_terms(spec_left, spec_right):
    real_part = jnp.einsum(
        "sim,som->iom", spec_left[:, :, 0], spec_right[:, :, 0], precision=HIGHEST
    )
    real_part = real_part + jnp.einsum(
        "sim,som->iom", spec_left[:, :, 1], spec_right[:, :, 1], precision=HIGHEST
    )
    imag_part = jnp.einsum(
        "sim,som->iom", spec_left[:, :, 0], spec_right[:, :, 1], precision=HIGHEST
    )
    imag_part = imag_part - jnp.einsum(
        "sim,som->iom", spec_left[:, :, 1], spec_right[:, :, 0], precision=HIGHEST
    )
    return jnp.stack([real_part, imag_part], axis=0)


def contract(weight_part, spec_part):
    return jnp.einsum("iom,som->sim", weight_part, spec_part, preferred_element_type=jnp.float32)


def skip_gradient(grid_in, cot_pre):
    partial_sum = jnp.einsum(
        "sixyz,soxyz->io", grid_in, cot_pre, preferred_element_type=jnp.float32
    )
    summed = lax.psum(partial_sum, ("batch", "space"))
    return summed / math.sqrt(grid_in.shape[0] * lax.axis_size("batch") * NX * NY * NZ)


def on_device(inputs, pre_act, cotangent, spectral_weight, skip_weight):
    samples = inputs.shape[0]
    channels = inputs.shape[1]
    slope_pre = gelu_slope(pre_act.astype(jnp.float32))
    cot_pre = (cotangent.astype(jnp.float32) * slope_pre).astype(jnp.bfloat16)
    spec_u, spec_e = both_along_y(
        (
            lax.all_to_all(
                local_spectrum(inputs), "space", split_axis=4, concat_axis=3, tiled=True
            ),
            lax.all_to_all(
                local_spectrum(cot_pre), "space", split_axis=4, concat_axis=3, tiled=True
            ),
        )
    )
    mode_count = spec_u.shape[3]
    position = jnp.arange(mode_count, dtype=jnp.int32)
    kxz_index = lax.axis_index("space") * (mode_count // (2 * MY)) + position // (2 * MY)
    mode_weights = jnp.where(kxz_index % MZ == 0, 1.0, 2.0).astype(jnp.float32) / float(
        NX * NY * NZ
    )
    mode_grad = lax.psum_scatter(
        cross_terms(spec_u, spec_e), "batch", scatter_dimension=2, tiled=True
    )
    grad_spectral = mode_grad * mode_weights
    rounded = spec_e.astype(jnp.bfloat16)
    weight_real = spectral_weight[0]
    weight_imag = spectral_weight[1]
    back_real = contract(weight_real, rounded[:, :, 0]) + contract(weight_imag, rounded[:, :, 1])
    back_imag = contract(weight_real, rounded[:, :, 1]) - contract(weight_imag, rounded[:, :, 0])
    back_modes = jnp.stack([back_real, back_imag], axis=2) * mode_weights
    shaped = back_modes.reshape(samples, channels, 2, mode_count // (2 * MY), 2 * MY)
    cos_y, sin_y = phase_table(NY, 2 * MY, True)
    grid_y = jnp.einsum("scpmk,pkqy->scqym", shaped, inverse_block(cos_y, sin_y), precision=HIGHEST)
    spatial = to_grid(lax.all_to_all(grid_y, "space", split_axis=3, concat_axis=4, tiled=True))
    mixed = jnp.einsum("io,soxyz->sixyz", skip_weight, cot_pre, preferred_element_type=jnp.float32)
    grad_inputs = (spatial + mixed).astype(jnp.bfloat16)
    grad_skip = skip_gradient(inputs, cot_pre)
    return (grad_inputs, grad_spectral, grad_skip)


def solution(mesh):
    placed = (
        P("batch", None, None, "space", None),
        P("batch", None, None, "space", None),
        P("batch", None, None, "space", None),
        P(None, None, None, "space"),
        P(),
    )
    return jax.shard_map(
        on_device,
        mesh=mesh,
        in_specs=placed,
        out_specs=(P("batch", None, None, "space", None), P(None, None, "batch", "space"), P()),
        check_vma=False,
    )
```

profile of v0, /device:TPU:1, one launch (start us, length us, event | category | flops | bytes accessed | tf_op | source)
XLA Modules:
  0.0 208.5 jit_solution(695585654018447)
XLA Ops:
  7.2 0.0 copy-start
  7.2 0.1 fusion.89
  7.3 0.1 fusion.84
  7.3 0.2 fusion.73
  7.5 2.3 %fusion.8 = bf16[1,32,128,1,128]{4,2,3,1,0:T(8,128)(2,1)S(1)} fusion(bf16[1,32,128,1,128]{4,2,3,1,0:T(8,128)(2,1)} %param.6, bf16[1,32,128,1,128]{4,2,3,1,0:T(8,128)(2,1)} %param.7), kind=kLoop, calls=%fused_computation.13 | loop fusion | flops 6291456 | bytes 3145728 | tf_op jit(solution)/shard_map/convert_element_type | solution.py:119
  9.8 0.3 convolution_bitcast_fusion.2
  10.1 2.5 %convolution_bitcast_fusion.4 = f32[1,32,2,1,32,16]{4,5,1,2,3,0:T(8,128)S(1)} fusion(f32[32,2,32,128]{3,2,0,1:T(8,128)S(1)} %convolution_bitcast_fusion.2, f32[1,128,2,16]{1,3,0,2:T(8,128)S(1)} %get-tuple-element.33, f32[1,128,2,16]{1,3,0,2:T(8,128)S(1)} %get-tuple-element.32), kind=kOutput, calls=%fused_computation.19 | convolution fusion | flops 100671488 | bytes 1212416 | tf_op jit(solution)/shard_map/scpayz,pzqk->scqyak/dot_general | solution.py:56
  12.6 0.4 copy.55
  12.9 0.4 copy.162
  13.3 1.2 reshape.693
  14.5 19.3 %all-to-all-start = ((f32[128,1,256]{2,1,0:T(1,128)}), f32[128,1,256]{2,1,0:T(1,128)S(1)}, u32[]{:S(2)}, u32[]{:S(2)}) async-start(f32[128,1,256]{2,1,0:T(1,128)} %reshape.693), calls=%async_computation | async-start | bytes 262144 | tf_op jit(solution)/shard_map/all_to_all | solution.py:125
  33.8 0.1 fusion.88
  33.9 0.1 fusion.86
  34.0 0.2 fusion.75
  34.1 0.0 copy-done
  34.1 0.3 convolution_bitcast_fusion.1
  34.4 0.0 copy-start.3
  34.5 2.5 %convolution_bitcast_fusion.3 = f32[1,32,2,1,32,16]{4,5,1,2,3,0:T(8,128)S(1)} fusion(f32[32,2,32,128]{3,2,0,1:T(8,128)S(1)} %convolution_bitcast_fusion.1, f32[1,128,2,16]{1,3,0,2:T(8,128)S(1)} %get-tuple-element.33, f32[1,128,2,16]{1,3,0,2:T(8,128)S(1)} %get-tuple-element.32), kind=kOutput, calls=%fused_computation.18 | convolution fusion | flops 100671488 | bytes 1212416 | tf_op jit(solution)/shard_map/scpayz,pzqk->scqyak/dot_general | solution.py:56
  36.9 1.3 convolution_bitcast_fusion.6
  38.2 2.1 fusion.18
  40.3 0.4 copy.69
  40.7 0.4 copy.161
  41.1 1.2 reshape.697
  42.3 98.4 %psum.7 = f32[32,32]{0,1:T(8,128)S(1)} all-reduce(f32[32,32]{0,1:T(8,128)S(1)} %convolution_bitcast_fusion.6), channel_id=1, replica_groups=mesh['batch'=4,'space'=128] {'batch','space'}, use_global_device_ids=true, to_apply=%region_1.2 | all-reduce | flops 1024 | bytes 8192 | tf_op jit(solution)/shard_map/psum | solution.py:111
  140.8 0.0 all-to-all-done
  140.8 10.2 %all-to-all-start.2 = ((f32[128,1,256]{2,1,0:T(1,128)}), f32[128,1,256]{2,1,0:T(1,128)S(1)}, u32[]{:S(2)}, u32[]{:S(2)}) async-start(f32[128,1,256]{2,1,0:T(1,128)} %reshape.697), calls=%async_computation.2 | async-start | bytes 262144 | tf_op jit(solution)/shard_map/all_to_all | solution.py:122
  151.0 0.0 reduce-scatter.2.cloned.1.call-start
  151.0 0.5 broadcast.824
  151.5 0.9 reduce.8
  152.5 0.4 reshape.694
  152.9 0.3 copy.59
  153.2 0.5 fusion.28
  153.7 0.1 copy.67
  153.8 0.1 copy.75
  153.8 9.4 %all-to-all-done.2 = f32[128,1,256]{2,1,0:T(1,128)S(1)} async-done(((f32[128,1,256]{2,1,0:T(1,128)}), f32[128,1,256]{2,1,0:T(1,128)S(1)}, u32[]{:S(2)}, u32[]{:S(2)}) %all-to-all-start.2) | async-done | bytes 131104 | tf_op jit(solution)/shard_map/all_to_all | solution.py:122
  163.2 0.9 reduce.10
  164.2 0.4 reshape.698
  164.6 0.3 copy.73
  164.9 0.5 fusion.25
  165.4 0.1 copy.74
  165.5 0.1 copy.76
  165.5 0.2 add_bitcast_fusion
  165.7 0.0 copy-start.2
  165.7 1.1 pad_maximum_fusion
  166.8 0.0 reduce-scatter.2.cloned.1.call-update
  166.9 0.1 copy.130
  166.9 0.1 copy.131
  167.0 0.4 fusion.22
  167.5 0.1 stack.145
  167.6 0.1 stack.144
  167.7 0.3 convolution_bitcast_fusion.5
  168.0 0.3 copy.61
  168.3 1.0 reshape.695
  169.3 6.4 %all-to-all-start.1 = ((f32[128,1,256]{2,1,0:T(1,128)}), f32[128,1,256]{2,1,0:T(1,128)S(1)}, u32[]{:S(2)}, u32[]{:S(2)}) async-start(f32[128,1,256]{2,1,0:T(1,128)} %reshape.695), calls=%async_computation.1 | async-start | bytes 262144 | tf_op jit(solution)/shard_map/all_to_all | solution.py:149
  175.7 0.7 copy.80
  176.4 0.2 fusion.79
  176.6 11.2 %all-to-all-done.1 = f32[128,1,256]{2,1,0:T(1,128)S(1)} async-done(((f32[128,1,256]{2,1,0:T(1,128)}), f32[128,1,256]{2,1,0:T(1,128)S(1)}, u32[]{:S(2)}, u32[]{:S(2)}) %all-to-all-start.1) | async-done | bytes 131104 | tf_op jit(solution)/shard_map/all_to_all | solution.py:149
  187.8 0.9 reduce.9
  188.8 1.0 reshape.696
  189.8 1.9 copy.62
  191.8 2.3 %copy.63 = f32[32,2,32,16]{2,3,1,0:T(8,128)} copy(f32[32,2,32,16]{0,3,2,1:T(8,128)} %bitcast.256) | data formatting | bytes 262144 | tf_op jit(solution)/shard_map/reshape.31
  194.0 2.1 convolution_bitcast_fusion
  196.1 3.9 %fusion.9 = bf16[1,32,128,1,128]{4,2,3,1,0:T(8,128)(2,1)} fusion(f32[128,128,32]{1,2,0:T(8,128)S(1)} %copy-done.1, f32[32,2,32,128]{3,2,0,1:T(8,128)S(1)} %convolution_bitcast_fusion, f32[1,32,128]{2,1,0:T(8,128)S(1)} %get-tuple-element.35, f32[1,32,128]{2,1,0:T(8,128)S(1)} %get-tuple-element.34), kind=kOutput, calls=%fused_computation.15 | convolution fusion | flops 403709952 | bytes 4227072 | tf_op jit(solution)/shard_map/scpayz,pax->scxyz/dot_general | solution.py:84
  200.0 1.7 broadcast_multiply_fusion
  (20 shorter events, 0.2 us)
Async XLA Ops:
  7.2 27.0 %copy-start = (bf16[1,32,128,1,128]{4,2,3,1,0:T(8,128)(2,1)S(1)}, bf16[1,32,128,1,128]{4,2,3,1,0:T(8,128)(2,1)}, u32[]{:S(2)}) copy-start(bf16[1,32,128,1,128]{4,2,3,1,0:T(8,128)(2,1)} %param.5) | copy-start | bytes 3145732
  14.5 126.2 %all-to-all-start = ((f32[128,1,256]{2,1,0:T(1,128)}), f32[128,1,256]{2,1,0:T(1,128)S(1)}, u32[]{:S(2)}, u32[]{:S(2)}) async-start(f32[128,1,256]{2,1,0:T(1,128)} %reshape.693), calls=%async_computation | async-start | bytes 262144 | tf_op jit(solution)/shard_map/all_to_all | solution.py:125
  34.4 3.8 %copy-start.3 = (bf16[32,32]{1,0:T(8,128)(2,1)S(1)}, bf16[32,32]{1,0:T(8,128)(2,1)}, u32[]{:S(2)}) copy-start(bf16[32,32]{1,0:T(8,128)(2,1)} %param.9) | copy-start | bytes 6148
  140.8 22.5 %all-to-all-start.2 = ((f32[128,1,256]{2,1,0:T(1,128)}), f32[128,1,256]{2,1,0:T(1,128)S(1)}, u32[]{:S(2)}, u32[]{:S(2)}) async-start(f32[128,1,256]{2,1,0:T(1,128)} %reshape.697), calls=%async_computation.2 | async-start | bytes 262144 | tf_op jit(solution)/shard_map/all_to_all | solution.py:122
  151.0 49.0 %reduce-scatter.2.cloned.1.call-start = ((), (), s32[]{:S(2)}) async-start(), calls=%async_computation.4 | async-start | bytes 1310720 | tf_op jit(solution)/shard_map/reduce_scatter | solution.py:136
  165.7 1.3 copy-start.2
  169.3 18.5 %all-to-all-start.1 = ((f32[128,1,256]{2,1,0:T(1,128)}), f32[128,1,256]{2,1,0:T(1,128)S(1)}, u32[]{:S(2)}, u32[]{:S(2)}) async-start(f32[128,1,256]{2,1,0:T(1,128)} %reshape.695), calls=%async_computation.1 | async-start | bytes 262144 | tf_op jit(solution)/shard_map/all_to_all | solution.py:149
  188.7 7.4 %copy-start.1 = (f32[128,128,32]{1,2,0:T(8,128)S(1)}, f32[128,128,32]{1,2,0:T(8,128)}, u32[]{:S(2)}) copy-start(f32[128,128,32]{1,2,0:T(8,128)} %fusion.18) | copy-start | bytes 6291460
Sparse Core Ops, SparseCore 0:
  166.9 32.9 reduce-scatter.1
where the time goes:
time: 210 us; the launch traced here: 208 us
  blocking collectives  98.4 us (47%)
  starting transfers between devices  35.9 us (17%)
  waiting for transfers between devices  20.7 us (10%)
  matrix products  16.1 us (8%)
  between operations  14.4 us (7%)
  local copies, waits for them, and re-layouts  13.8 us (7%)
  other arithmetic  9.26 us (4%)
    psum x1, blocking collectives, skip_gradient(): summed = lax.psum(partial_sum, ('batch', 'space'))  98.4 us
    all_to_all x1, starting transfers between devices, on_device(): lax.all_to_all(local_spectrum(cot_pre), 'space', split_axis=4, concat_axi...  19.3 us
    all_to_all x1, waiting for transfers between devices, on_device(): lax.all_to_all(grid_y, 'space', split_axis=3, concat_axis=4, tiled=True)  11.2 us
    all_to_all x1, starting transfers between devices, on_device(): lax.all_to_all(local_spectrum(inputs), 'space', split_axis=4, concat_axis...  10.2 us
    all_to_all x1, waiting for transfers between devices, on_device(): lax.all_to_all(local_spectrum(inputs), 'space', split_axis=4, concat_axis...  9.4 us
    all_to_all x1, starting transfers between devices, on_device(): lax.all_to_all(grid_y, 'space', split_axis=3, concat_axis=4, tiled=True)  6.39 us
    unnamed x17, local copies, waits for them, and re-layouts  6.13 us
    dot_general x2, matrix products, local_spectrum(): jnp.einsum('scpayz,pzqk->scqyak', section_x, forward_block(cos_z, sin_z),...  4.95 us
  transfers between devices with their start and end apart: 4, of which 2 were waited for; matrix products, arithmetic and copies ran while one was open for 13% of the time, Pallas kernels for 0%

commit v1 on v0

v1 whole, which is shorter than its diff:
```python
import math

import jax
import jax.numpy as jnp
import ml_dtypes
import numpy as np
from jax import lax
from jax.experimental import pallas as pl
from jax.experimental.pallas import tpu as pltpu
from jax.sharding import PartitionSpec as P

N = 128
MODES = 32
BATCH = 4
CHANNELS = 32
F32 = jnp.float32
BF16 = jnp.bfloat16
MESH = pl.DeviceIdType.MESH


def signed(index):
    return np.where(index < 16, index, index - 32)


def phases(points, orders):
    angles = np.mod(points[:, None] * orders[None, :], N) * (2.0 * math.pi / N)
    return np.cos(angles), np.sin(angles)


def bf16(table):
    return table.astype(np.float32).astype(ml_dtypes.bfloat16)


def places():
    t = np.arange(16)
    return t // 4, t // 2 % 2, t % 2


def make_tables():
    points = np.arange(N)
    eye = np.eye(8)
    cos_z, sin_z = (v.reshape(N, 4, 4) for v in phases(points, np.arange(16)))
    fwd_z = np.stack([np.einsum("zqk,cd->czqdk", v, eye) for v in (cos_z, -sin_z)], axis=2)
    fwd_z = fwd_z.reshape(8 * N, 256)
    inv_z = np.stack([np.einsum("zqk,cd->qckdz", v, eye) for v in (cos_z, -sin_z)], axis=0)
    inv_z = inv_z.reshape(256, 8 * N)
    cos_x, sin_x = phases(points, signed(np.arange(32)))
    cos_x, sin_x = bf16(cos_x).astype(np.float64), bf16(sin_x).astype(np.float64)
    parts = np.stack([np.stack([cos_x, sin_x]), np.stack([-sin_x, cos_x])])
    parts = parts.reshape(2, 2, N, 2, 8, 2)
    fwd_x = np.transpose(parts, (3, 5, 0, 4, 1, 2)).reshape(64, 256)
    cos_x, sin_x = phases(points, signed(np.arange(32)))
    parts = np.stack([np.stack([cos_x, -sin_x]), np.stack([sin_x, cos_x])]).reshape(2, 2, N, 2, 8, 2)
    inv_x = np.transpose(parts, (0, 2, 4, 3, 5, 1)).reshape(256, 64)
    q, a, h = places()
    y = a[None, :] * 64 + np.arange(8)[:, None] * 8 + h[None, :] * 4 + q[None, :]
    cos_y, sin_y = phases(y.reshape(-1), signed(np.arange(32)))
    cos_y, sin_y = cos_y.reshape(8, 16, 32), sin_y.reshape(8, 16, 32)
    parts = np.stack([np.stack([cos_y, sin_y]), np.stack([-sin_y, cos_y])])
    fwd_y = np.transpose(parts, (2, 3, 1, 0, 4))[:, :, :, :, None, :]
    fwd_y = np.broadcast_to(fwd_y, (8, 16, 2, 2, 4, 32)).reshape(256, 256)
    parts = np.stack([np.stack([cos_y, -sin_y]), np.stack([sin_y, cos_y])])
    inv_y = np.transpose(parts, (3, 0, 2, 1, 4))[:, :, :, :, None, :]
    inv_y = np.broadcast_to(inv_y, (16, 2, 8, 2, 4, 32)).reshape(256, 256)
    return tuple(bf16(v) for v in (fwd_z, fwd_x, fwd_y, inv_y, inv_x, inv_z))


def gelu_slope(values):
    normal_cdf = 0.5 * (1.0 + lax.erf(values * (1.0 / math.sqrt(2.0))))
    density = jnp.exp(-0.5 * values * values) * (1.0 / math.sqrt(2.0 * math.pi))
    return normal_cdf + values * density


def dot(left, right):
    return jnp.dot(left, right, preferred_element_type=F32)


def lanes(blocks):
    return jnp.concatenate(blocks, axis=1)


def to_modes(field, table_z, table_x, sent):
    sections = []
    for g in range(4):
        along_z = dot(lanes([field[8 * g + j] for j in range(8)]), table_z[...])
        both = jnp.concatenate([along_z[:, :N], along_z[:, N:]], axis=0).astype(BF16)
        sections.append(dot(table_x[...], both))
    for q in range(4):
        sent[64 * q : 64 * q + 64, :] = lanes([v[:, 32 * q : 32 * q + 32] for v in sections])


def turn(received, sent):
    for b in range(8):
        sent[b] = received[pl.ds(b, 32, stride=8), :]


def k4_lanes(rows):
    return lax.broadcasted_iota(jnp.int32, (rows, N), 1) // 32


def along_y(received, table_y, rows, put):
    both = lax.dot_general(
        received[...].reshape(256, N).astype(BF16),
        table_y[...],
        (((0,), (0,)), ((), ())),
        preferred_element_type=F32,
    )
    block = k4_lanes(32)
    for part in range(2):
        rows[part] = both[:, N * part : N * part + N]
        value = rows[part, pl.ds(0, 32, stride=4), :]
        for k4 in range(1, 4):
            value = jnp.where(block == k4, rows[part, pl.ds(k4, 32, stride=4), :], value)
        put(part, value)


def kernel(
    in_hbm, pre_hbm, cot_hbm, weight_hbm, skip_hbm,
    fz_hbm, fx_hbm, fy_hbm, iy_hbm, ix_hbm, iz_hbm,
    out_hbm, spectral_hbm, mixgrad_hbm,
    v_in, v_pre, v_cot, v_weight, v_skip, fz, fx, fy, iy, ix, iz,
    v_cp, v_mix, v_out, v_spectral, v_mixgrad,
    u_send, u_mid, u_turn, u_all, e_send, e_mid, e_turn, e_all, g_send, g_mid, g_turn, g_all,
    u_own, u_batch, e_own, e_batch, rows, partial, back_rows,
    prod, prod_rows, kron, skip_rows, m_own, m_one, m_two_own, m_two, m_three_own, m_three,
    load_sem, out_sem, send_sem, recv_sem,
):
    loads = [
        pltpu.make_async_copy(src, dst, load_sem.at[n])
        for n, (src, dst) in enumerate(
            (
                (in_hbm, v_in), (fz_hbm, fz), (fx_hbm, fx), (pre_hbm, v_pre), (cot_hbm, v_cot),
                (skip_hbm, v_skip), (fy_hbm, fy), (weight_hbm, v_weight), (iy_hbm, iy),
                (ix_hbm, ix), (iz_hbm, iz),
            )
        )
    ]
    for copy in loads:
        copy.start()

    sample = lax.axis_index("batch")
    place = lax.axis_index("space")
    a = place // 64
    b = place // 8 % 8
    h = place // 4 % 2
    q = place % 4
    t = 4 * q + 2 * a + h

    def near(k):
        peer = (t + k) % 16
        return peer, peer // 2 % 2 * 64 + b * 8 + peer % 2 * 4 + peer // 4

    def far(k):
        peer = (b + k) % 8
        return peer, a * 64 + peer * 8 + h * 4 + q

    def other(k):
        return (sample + k) % BATCH

    barrier = pltpu.get_barrier_semaphore()

    @pl.loop(1, 16)
    def _(k):
        pl.semaphore_signal(barrier, inc=1, device_id={"space": near(k)[1]}, device_id_type=MESH)

    @pl.loop(1, 8)
    def _(k):
        pl.semaphore_signal(barrier, inc=1, device_id={"space": far(k)[1]}, device_id_type=MESH)

    @pl.loop(1, BATCH)
    def _(k):
        pl.semaphore_signal(barrier, inc=1, device_id={"batch": other(k)}, device_id_type=MESH)

    def remote(src, dst, n, where):
        return pltpu.make_async_remote_copy(
            src_ref=src, dst_ref=dst, send_sem=send_sem.at[n], recv_sem=recv_sem.at[n],
            device_id=where, device_id_type=MESH,
        )

    def rows16(ref, slot):
        return ref.at[pl.ds(pl.multiple_of(slot * 16, 16), 16), :]

    def send_near(src, dst, n):
        pltpu.make_async_copy(rows16(src, t), rows16(dst, t), recv_sem.at[n]).start()

        @pl.loop(1, 16)
        def _(k):
            peer, where = near(k)
            remote(rows16(src, peer), rows16(dst, t), n, {"space": where}).start()

    def send_far(src, dst, n):
        pltpu.make_async_copy(src.at[b], dst.at[b], recv_sem.at[n]).start()

        @pl.loop(1, 8)
        def _(k):
            peer, where = far(k)
            remote(src.at[peer], dst.at[b], n, {"space": where}).start()

    def send_batch(src, dst, n):
        pltpu.make_async_copy(src, dst.at[sample], recv_sem.at[n]).start()

        @pl.loop(1, BATCH)
        def _(k):
            remote(src, dst.at[sample], n, {"batch": other(k)}).start()

    def arrived(ref, n):
        pltpu.make_async_copy(ref, ref, recv_sem.at[n]).wait()

    def left(ref, n):
        pltpu.make_async_copy(ref, ref, send_sem.at[n]).wait()

    for n in range(3):
        loads[n].wait()
    to_modes(v_in, fz, fx, u_send)
    pl.semaphore_wait(barrier, 15 + 7 + BATCH - 1)
    send_near(u_send, u_mid, 0)

    loads[3].wait()
    loads[4].wait()

    @pl.loop(0, CHANNELS)
    def _(c):
        slope = gelu_slope(v_pre[c].astype(F32))
        v_cp[c] = (v_cot[c].astype(F32) * slope).astype(BF16)

    to_modes(v_cp, fz, fx, e_send)
    send_near(e_send, e_mid, 1)
    arrived(u_mid, 0)
    turn(u_mid, u_turn)
    send_far(u_turn, u_all, 2)

    loads[5].wait()
    chunks = range(8)
    prod[...] = lax.dot_general(
        lanes([v_in[:, 16 * j : 16 * j + 16, :].reshape(512, N) for j in chunks]),
        lanes([v_cp[:, 16 * j : 16 * j + 16, :].reshape(512, N) for j in chunks]),
        (((1,), (1,)), ((), ())),
        preferred_element_type=F32,
    )
    row16 = lax.broadcasted_iota(jnp.int32, (16, 512), 0)
    column = lax.broadcasted_iota(jnp.int32, (16, 512), 1)
    same = row16 == column % 16
    for i in range(CHANNELS):
        kept = jnp.where(same, prod[16 * i : 16 * i + 16, :], 0.0)
        kept = kept[:8] + kept[8:]
        for n in range(4):
            prod_rows[n, 8 * i : 8 * i + 8, :] = kept[:, N * n : N * n + N]
    summed = []
    for n in range(4):
        value = prod_rows[n, pl.ds(0, 32, stride=8), :]
        for j in range(1, 8):
            value = value + prod_rows[n, pl.ds(j, 32, stride=8), :]
        summed.append(value)
    summed = lanes(summed)
    wide = lax.broadcasted_iota(jnp.int32, (512, 32), 0) // 16
    spread = wide == lax.broadcasted_iota(jnp.int32, (512, 32), 1)
    own = jnp.dot(
        summed, spread.astype(F32), precision=lax.Precision.HIGHEST, preferred_element_type=F32
    )
    m_own[...] = lanes([own[8 * r : 8 * r + 8, :] for r in range(4)])

    pltpu.make_async_copy(m_own, m_one.at[t], recv_sem.at[3]).start()

    @pl.loop(1, 16)
    def _(k):
        remote(m_own, m_one.at[t], 3, {"space": near(k)[1]}).start()

    arrived(e_mid, 1)
    turn(e_mid, e_turn)
    send_far(e_turn, e_all, 4)

    tall = lax.broadcasted_iota(jnp.int32, (32, 512), 1) // 16
    spread_t = tall == lax.broadcasted_iota(jnp.int32, (32, 512), 0)
    repeated = dot(v_skip[...], spread_t.astype(F32).astype(BF16))
    for n in range(4):
        skip_rows[n] = repeated[:, N * n : N * n + N]
    for i in range(CHANNELS):
        row = lanes([skip_rows[n, pl.ds(i, 16, stride=0), :] for n in range(4)])
        kron[16 * i : 16 * i + 16, :] = jnp.where(same, row, 0.0).astype(BF16)
    for j in range(0, 8, 2):
        pair = [v_cp[:, 16 * n : 16 * n + 16, :].reshape(512, N) for n in (j, j + 1)]
        mixed = dot(kron[...], lanes(pair))
        for n in range(2):
            v_mix[:, 16 * (j + n) : 16 * (j + n) + 16, :] = mixed[:, N * n : N * n + N].reshape(
                32, 16, N
            )

    arrived(u_all, 2)
    loads[6].wait()

    def put_u(part, value):
        u_own[32 * part : 32 * part + 32, :] = value

    along_y(u_all, fy, rows, put_u)
    send_batch(u_own, u_batch, 5)

    arrived(e_all, 4)
    e_rounded = []

    def put_e(part, value):
        for block in range(4):
            e_own[block, 8 * part : 8 * part + 8, :] = value[8 * block : 8 * block + 8, :]
        e_rounded.append(value.astype(BF16).astype(F32))

    along_y(e_all, fy, rows, put_e)

    loads[7].wait()
    e_real, e_imag = e_rounded
    for i in range(CHANNELS):
        w_real = v_weight[0, i].astype(F32)
        w_imag = v_weight[1, i].astype(F32)
        real = w_real * e_real + w_imag * e_imag
        imag = w_real * e_imag - w_imag * e_real
        for part, value in enumerate((real, imag)):
            partial[part, 8 * i : 8 * i + 8, :] = (
                value[0:8] + value[8:16] + (value[16:24] + value[24:32])
            )
    lane = lax.broadcasted_iota(jnp.int32, (1, N), 1)
    zero_kz = jnp.logical_and(q == 0, lane < 32)
    scale = jnp.where(zero_kz, 1.0, 2.0).astype(F32) / float(N * N * N)
    block = k4_lanes(32)
    for part in range(2):
        value = partial[part, pl.ds(0, 32, stride=8), :]
        for j in range(1, 8):
            value = value + partial[part, pl.ds(j, 32, stride=8), :]
        value = value * scale
        for k4 in range(4):
            back_rows[part, pl.ds(k4, 32, stride=4), :] = jnp.where(block == k4, value, 0.0)
    loads[8].wait()
    g_send[...] = lax.dot_general(
        iy[...],
        lanes([back_rows[0], back_rows[1]]).astype(BF16),
        (((1,), (1,)), ((), ())),
        preferred_element_type=F32,
    )
    send_near(g_send, g_mid, 6)

    pltpu.make_async_copy(e_own.at[sample], e_batch.at[sample], recv_sem.at[7]).start()

    @pl.loop(1, BATCH)
    def _(k):
        peer = other(k)
        remote(e_own.at[peer], e_batch.at[sample], 7, {"batch": peer}).start()

    arrived(m_one, 3)
    total = m_one[0]
    for n in range(1, 16):
        total = total + m_one[n]
    m_two_own[...] = total
    pltpu.make_async_copy(m_two_own, m_two.at[b], recv_sem.at[8]).start()

    @pl.loop(1, 8)
    def _(k):
        remote(m_two_own, m_two.at[b], 8, {"space": far(k)[1]}).start()

    arrived(g_mid, 6)
    turn(g_mid, g_turn)
    send_far(g_turn, g_all, 9)

    arrived(u_batch, 5)
    arrived(e_batch, 7)
    for i in range(CHANNELS):
        real = jnp.zeros((8, N), F32)
        imag = jnp.zeros((8, N), F32)
        for n in range(BATCH):
            u_real = u_batch[n, pl.ds(i, 8, stride=0), :]
            u_imag = u_batch[n, pl.ds(32 + i, 8, stride=0), :]
            e_r = e_batch[n, 0:8, :]
            e_i = e_batch[n, 8:16, :]
            real = real + (u_real * e_r + u_imag * e_i)
            imag = imag + (u_real * e_i - u_imag * e_r)
        v_spectral[0, i] = real * scale
        v_spectral[1, i] = imag * scale
    spectral_copy = pltpu.make_async_copy(v_spectral, spectral_hbm, out_sem.at[4])
    spectral_copy.start()

    arrived(m_two, 8)
    total = m_two[0]
    for n in range(1, 8):
        total = total + m_two[n]
    m_three_own[...] = total
    send_batch(m_three_own, m_three, 10)

    loads[9].wait()
    loads[10].wait()
    arrived(g_all, 9)
    outs = []
    for g in range(4):
        spectra = lanes(
            [
                g_all[:, 8 * n : 8 * n + 8, 32 * g : 32 * g + 32].reshape(64, 32)
                for n in range(4)
            ]
        )
        along_x = dot(ix[...], spectra.astype(BF16))
        both = lanes([along_x[:N], along_x[N:]]).astype(BF16)
        for n in range(4):
            grid = dot(both, iz[:, 256 * n : 256 * n + 256])
            for r in range(2):
                i = 8 * g + 2 * n + r
                v_out[i] = (grid[:, N * r : N * r + N] + v_mix[i]).astype(BF16)
        copy = pltpu.make_async_copy(
            v_out.at[8 * g : 8 * g + 8], out_hbm.at[8 * g : 8 * g + 8], out_sem.at[g]
        )
        copy.start()
        outs.append(copy)

    arrived(m_three, 10)
    total = (m_three[0] + m_three[1] + (m_three[2] + m_three[3])) / math.sqrt(BATCH * N * N * N)
    for r in range(4):
        v_mixgrad[8 * r : 8 * r + 8, :] = total[:, 32 * r : 32 * r + 32]
    mixgrad_copy = pltpu.make_async_copy(v_mixgrad, mixgrad_hbm, out_sem.at[5])
    mixgrad_copy.start()

    left(u_send.at[0:240], 0)
    left(e_send.at[0:240], 1)
    left(u_turn.at[0:7], 2)
    left(m_one.at[0:15], 3)
    left(e_turn.at[0:7], 4)
    left(u_batch.at[0:3], 5)
    left(g_send.at[0:240], 6)
    left(e_own.at[0:3], 7)
    left(m_two.at[0:7], 8)
    left(g_turn.at[0:7], 9)
    left(m_three.at[0:3], 10)
    for copy in outs:
        copy.wait()
    spectral_copy.wait()
    mixgrad_copy.wait()


def on_device(inputs, pre_act, cotangent, spectral_weight, skip_weight):
    field = (CHANNELS, N, N)
    tables = [jnp.asarray(v) for v in make_tables()]
    exchange = [
        pltpu.VMEM((256, N), F32), pltpu.VMEM((256, N), F32),
        pltpu.VMEM((8, 32, N), F32), pltpu.VMEM((8, 32, N), F32),
    ]
    anywhere = pl.BlockSpec(memory_space=pl.ANY)
    grad_inputs, grad_spectral, grad_skip = pl.pallas_call(
        kernel,
        out_shape=(
            jax.ShapeDtypeStruct(field, BF16),
            jax.ShapeDtypeStruct((2, CHANNELS, 8, N), F32),
            jax.ShapeDtypeStruct((CHANNELS, CHANNELS), F32),
        ),
        in_specs=[anywhere] * 11,
        out_specs=(anywhere,) * 3,
        scratch_shapes=[
            pltpu.VMEM(field, BF16), pltpu.VMEM(field, BF16), pltpu.VMEM(field, BF16),
            pltpu.VMEM((2, 32, 32, N), BF16), pltpu.VMEM((32, 32), BF16),
            *(pltpu.VMEM(v.shape, BF16) for v in tables),
            pltpu.VMEM(field, BF16), pltpu.VMEM(field, F32), pltpu.VMEM(field, BF16),
            pltpu.VMEM((2, 32, 8, N), F32), pltpu.VMEM((32, 32), F32),
            *exchange, *exchange, *exchange,
            pltpu.VMEM((64, N), F32), pltpu.VMEM((BATCH, 64, N), F32),
            pltpu.VMEM((4, 16, N), F32), pltpu.VMEM((BATCH, 16, N), F32),
            pltpu.VMEM((2, N, N), F32), pltpu.VMEM((2, 256, N), F32), pltpu.VMEM((2, N, N), F32),
            pltpu.VMEM((512, 512), F32), pltpu.VMEM((4, 256, N), F32),
            pltpu.VMEM((512, 512), BF16), pltpu.VMEM((4, 32, N), F32),
            pltpu.VMEM((8, N), F32), pltpu.VMEM((16, 8, N), F32),
            pltpu.VMEM((8, N), F32), pltpu.VMEM((8, 8, N), F32),
            pltpu.VMEM((8, N), F32), pltpu.VMEM((BATCH, 8, N), F32),
            pltpu.SemaphoreType.DMA((11,)), pltpu.SemaphoreType.DMA((6,)),
            pltpu.SemaphoreType.DMA((11,)), pltpu.SemaphoreType.DMA((11,)),
        ],
        compiler_params=pltpu.CompilerParams(
            collective_id=0, has_side_effects=True, vmem_limit_bytes=48 * 2**20
        ),
    )(
        inputs.reshape(field), pre_act.reshape(field), cotangent.reshape(field),
        spectral_weight, skip_weight, *tables,
    )
    return grad_inputs.reshape(inputs.shape), grad_spectral, grad_skip


def solution(mesh):
    placed = (
        P("batch", None, None, "space", None),
        P("batch", None, None, "space", None),
        P("batch", None, None, "space", None),
        P(None, None, None, "space"),
        P(),
    )
    return jax.shard_map(
        on_device,
        mesh=mesh,
        in_specs=placed,
        out_specs=(P("batch", None, None, "space", None), P(None, None, "batch", "space"), P()),
        check_vma=False,
    )
```

time: 210 us -> 56.3 us (0.27)
  blocking collectives: 98.4 us -> 0 us
  Pallas kernels: 0 us -> 42.8 us
  starting transfers between devices: 35.9 us -> 0 us
  waiting for transfers between devices: 20.7 us -> 0 us
  matrix products: 16.1 us -> 0 us
  between operations: 14.4 us -> 0.66 us
  other arithmetic: 9.26 us -> 0 us
    psum x1 -> x0, blocking collectives: 98.4 us -> none  [skip_gradient(): summed = lax.psum(partial_sum, ('batch', 'space'))]
    pallas_call x0 -> x1, Pallas kernels: none -> 42.8 us  [on_device(): pl.pallas_call(kernel, out_shape=(jax.ShapeDtypeStruct(field, BF16), jax....]
    all_to_all x3 -> x0, starting transfers between devices: 35.9 us -> none  [the longest x1 19.3 us: on_device(): lax.all_to_all(local_spectrum(cot_pre), 'space', split_axis=4, concat_axi...]
    all_to_all x3 -> x0, waiting for transfers between devices: 20.6 us -> none  [the longest x1 11.2 us: on_device(): lax.all_to_all(grid_y, 'space', split_axis=3, concat_axis=4, tiled=True)]
    dot_general x11 -> x0, matrix products: 16.1 us -> none  [the longest x2 4.95 us: local_spectrum(): jnp.einsum('scpayz,pzqk->scqyak', section_x, forward_block(cos_z, sin_z),...]
    unnamed x17 -> x23, local copies, waits for them, and re-layouts: 6.13 us -> 11.9 us
    another operation x11 -> x0, local copies, waits for them, and re-layouts: 3.38 us -> none
    all_to_all x3 -> x0, other arithmetic: 2.77 us -> none  [the longest x1 0.92 us: on_device(): lax.all_to_all(local_spectrum(inputs), 'space', split_axis=4, concat_axis...]
  transfers between devices with their start and end apart: 4 -> 0, of which waited for: 2 -> 0; matrix products, arithmetic and copies ran while one was open for 13% -> 0% of each run, Pallas kernels for 0% -> 0%
where the time goes in v1:
time: 56.3 us; the launch traced here: 55.4 us
  Pallas kernels  42.8 us (76%)
  local copies, waits for them, and re-layouts  11.9 us (21%)
  between operations  0.66 us (1%)
    pallas_call x1, Pallas kernels, on_device(): pl.pallas_call(kernel, out_shape=(jax.ShapeDtypeStruct(field, BF16), jax....  42.8 us
    unnamed x23, local copies, waits for them, and re-layouts  11.9 us

profile of v1, /device:TPU:1, one launch (start us, length us, event | category | flops | bytes accessed | tf_op | source)
XLA Modules:
  0.0 55.4 jit_solution(6464847347171447030)
XLA Ops:
  0.6 0.0 copy-start
  0.6 1.2 %copy-done = bf16[1,32,128,1,128]{4,2,3,1,0:T(8,128)(2,1)S(1)} copy-done((bf16[1,32,128,1,128]{4,2,3,1,0:T(8,128)(2,1)S(1)}, bf16[1,32,128,1,128]{4,2,3,1,0:T(8,128)(2,1)}, u32[]{:S(2)}) %copy-start) | copy-done | bytes 1048600
  1.9 0.0 copy-start.1
  1.9 1.2 %copy-done.1 = bf16[1,32,128,1,128]{4,2,3,1,0:T(8,128)(2,1)S(1)} copy-done((bf16[1,32,128,1,128]{4,2,3,1,0:T(8,128)(2,1)S(1)}, bf16[1,32,128,1,128]{4,2,3,1,0:T(8,128)(2,1)}, u32[]{:S(2)}) %copy-start.1) | copy-done | bytes 1048600
  3.1 0.0 copy-start.2
  3.1 1.0 %copy-done.2 = bf16[2,32,32,128]{3,2,1,0:T(8,128)(2,1)S(1)} copy-done((bf16[2,32,32,128]{3,2,1,0:T(8,128)(2,1)S(1)}, bf16[2,32,32,128]{3,2,1,0:T(8,128)(2,1)}, u32[]{:S(2)}) %copy-start.2) | copy-done | bytes 524312
  4.1 0.0 copy-start.3
  4.1 1.0 %copy-done.3 = bf16[256,1024]{1,0:T(8,128)(2,1)S(1)} copy-done((bf16[256,1024]{1,0:T(8,128)(2,1)S(1)}, bf16[256,1024]{1,0:T(8,128)(2,1)}, u32[]{:S(2)}) %copy-start.3) | copy-done | bytes 524312
  5.2 0.0 copy-start.4
  5.2 1.0 %copy-done.4 = bf16[1024,256]{1,0:T(8,128)(2,1)S(1)} copy-done((bf16[1024,256]{1,0:T(8,128)(2,1)S(1)}, bf16[1024,256]{1,0:T(8,128)(2,1)}, u32[]{:S(2)}) %copy-start.4) | copy-done | bytes 524312
  6.2 0.0 copy-start.5
  6.2 0.9 %copy-done.5 = bf16[256,256]{1,0:T(8,128)(2,1)S(1)} copy-done((bf16[256,256]{1,0:T(8,128)(2,1)S(1)}, bf16[256,256]{1,0:T(8,128)(2,1)}, u32[]{:S(2)}) %copy-start.5) | copy-done | bytes 131096
  7.1 0.0 copy-start.6
  7.1 0.9 %copy-done.6 = bf16[256,256]{1,0:T(8,128)(2,1)S(1)} copy-done((bf16[256,256]{1,0:T(8,128)(2,1)S(1)}, bf16[256,256]{1,0:T(8,128)(2,1)}, u32[]{:S(2)}) %copy-start.6) | copy-done | bytes 131096
  8.0 0.0 copy-start.7
  8.0 0.8 %copy-done.7 = bf16[256,64]{1,0:T(8,128)(2,1)S(1)} copy-done((bf16[256,64]{1,0:T(8,128)(2,1)S(1)}, bf16[256,64]{1,0:T(8,128)(2,1)}, u32[]{:S(2)}) %copy-start.7) | copy-done | bytes 32792
  8.9 0.0 copy-start.8
  8.9 0.8 %copy-done.8 = bf16[64,256]{1,0:T(8,128)(2,1)S(1)} copy-done((bf16[64,256]{1,0:T(8,128)(2,1)S(1)}, bf16[64,256]{1,0:T(8,128)(2,1)}, u32[]{:S(2)}) %copy-start.8) | copy-done | bytes 32792
  9.6 0.0 copy-start.9
  9.6 0.7 %copy-done.9 = bf16[32,32]{1,0:T(8,128)(2,1)S(1)} copy-done((bf16[32,32]{1,0:T(8,128)(2,1)S(1)}, bf16[32,32]{1,0:T(8,128)(2,1)}, u32[]{:S(2)}) %copy-start.9) | copy-done | bytes 2072
  10.3 42.8 %shard_map.130 = (bf16[32,128,128]{2,1,0:T(8,128)(2,1)S(1)}, f32[2,32,8,128]{3,2,1,0:T(8,128)S(1)}, f32[32,32]{1,0:T(8,128)S(1)}) custom-call(bf16[32,128,128]{2,1,0:T(8,128)(2,1)S(1)} %bitcast.6, bf16[32,128,128]{2,1,0:T(8,128)(2,1)S(1)} %bitcast.7, bf16[32,128,128]{2,1,0:T(8,128)(2,1)} %bitcast.9, bf16[2,32,32,128]{3,2,1,0:T(8,128)(2,1)S(1)} %copy-done.2, ...), custom_call_target="tpu_custom_call" | custom-call | tf_op jit(solution)/shard_map/pallas_call | solution.py:440
  53.2 1.0 %copy.18 = bf16[1,32,128,1,128]{4,2,3,1,0:T(8,128)(2,1)} copy(bf16[1,32,128,1,128]{4,2,3,1,0:T(8,128)(2,1)S(1)} %bitcast.8) | data formatting | bytes 2097152
  54.1 0.7 %copy.19 = f32[2,32,8,128]{3,2,1,0:T(8,128)} copy(f32[2,32,8,128]{3,2,1,0:T(8,128)S(1)} %get-tuple-element.16) | data formatting | bytes 524288
  54.8 0.6 %copy.20 = f32[32,32]{1,0:T(8,128)} copy(f32[32,32]{1,0:T(8,128)S(1)} %get-tuple-element.17) | data formatting | bytes 8192
Async XLA Ops:
  0.6 1.2 %copy-start = (bf16[1,32,128,1,128]{4,2,3,1,0:T(8,128)(2,1)S(1)}, bf16[1,32,128,1,128]{4,2,3,1,0:T(8,128)(2,1)}, u32[]{:S(2)}) copy-start(bf16[1,32,128,1,128]{4,2,3,1,0:T(8,128)(2,1)} %param.11) | copy-start | bytes 3145732
  1.9 1.2 %copy-start.1 = (bf16[1,32,128,1,128]{4,2,3,1,0:T(8,128)(2,1)S(1)}, bf16[1,32,128,1,128]{4,2,3,1,0:T(8,128)(2,1)}, u32[]{:S(2)}) copy-start(bf16[1,32,128,1,128]{4,2,3,1,0:T(8,128)(2,1)} %param.12) | copy-start | bytes 3145732
  3.1 1.0 %copy-start.2 = (bf16[2,32,32,128]{3,2,1,0:T(8,128)(2,1)S(1)}, bf16[2,32,32,128]{3,2,1,0:T(8,128)(2,1)}, u32[]{:S(2)}) copy-start(bf16[2,32,32,128]{3,2,1,0:T(8,128)(2,1)} %weight_hbm.1) | copy-start | bytes 1572868
  4.1 1.0 %copy-start.3 = (bf16[256,1024]{1,0:T(8,128)(2,1)S(1)}, bf16[256,1024]{1,0:T(8,128)(2,1)}, u32[]{:S(2)}) copy-start(bf16[256,1024]{1,0:T(8,128)(2,1)} %constant.17.clone.iz_hbm) | copy-start | bytes 1572868
  5.2 1.0 %copy-start.4 = (bf16[1024,256]{1,0:T(8,128)(2,1)S(1)}, bf16[1024,256]{1,0:T(8,128)(2,1)}, u32[]{:S(2)}) copy-start(bf16[1024,256]{1,0:T(8,128)(2,1)} %constant.12.clone.fz_hbm) | copy-start | bytes 1572868
  6.2 0.9 %copy-start.5 = (bf16[256,256]{1,0:T(8,128)(2,1)S(1)}, bf16[256,256]{1,0:T(8,128)(2,1)}, u32[]{:S(2)}) copy-start(bf16[256,256]{1,0:T(8,128)(2,1)} %constant.15.clone.iy_hbm) | copy-start | bytes 393220
  7.1 0.9 %copy-start.6 = (bf16[256,256]{1,0:T(8,128)(2,1)S(1)}, bf16[256,256]{1,0:T(8,128)(2,1)}, u32[]{:S(2)}) copy-start(bf16[256,256]{1,0:T(8,128)(2,1)} %constant.14.clone.fy_hbm) | copy-start | bytes 393220
  8.0 0.8 %copy-start.7 = (bf16[256,64]{1,0:T(8,128)(2,1)S(1)}, bf16[256,64]{1,0:T(8,128)(2,1)}, u32[]{:S(2)}) copy-start(bf16[256,64]{1,0:T(8,128)(2,1)} %constant.16.clone.ix_hbm) | copy-start | bytes 98308
  8.9 0.8 %copy-start.8 = (bf16[64,256]{1,0:T(8,128)(2,1)S(1)}, bf16[64,256]{1,0:T(8,128)(2,1)}, u32[]{:S(2)}) copy-start(bf16[64,256]{1,0:T(8,128)(2,1)} %constant.13.clone.fx_hbm) | copy-start | bytes 98308
  9.6 0.7 %copy-start.9 = (bf16[32,32]{1,0:T(8,128)(2,1)S(1)}, bf16[32,32]{1,0:T(8,128)(2,1)}, u32[]{:S(2)}) copy-start(bf16[32,32]{1,0:T(8,128)(2,1)} %skip_hbm.1) | copy-start | bytes 6148

commit v2 on v1

--- a/solution.py
+++ b/solution.py
@@ -29,6 +29,11 @@
 
 def bf16(table):
     return table.astype(np.float32).astype(ml_dtypes.bfloat16)
+
+
+def split(table):
+    high = bf16(table)
+    return high, bf16(table - high.astype(np.float64))
 
 
 def places():
@@ -62,7 +67,10 @@
     parts = np.stack([np.stack([cos_y, -sin_y]), np.stack([sin_y, cos_y])])
     inv_y = np.transpose(parts, (3, 0, 2, 1, 4))[:, :, :, :, None, :]
     inv_y = np.broadcast_to(inv_y, (16, 2, 8, 2, 4, 32)).reshape(256, 256)
-    return tuple(bf16(v) for v in (fwd_z, fwd_x, fwd_y, inv_y, inv_x, inv_z))
+    inv_x_high, inv_x_low = split(inv_x)
+    inv_x = np.concatenate([inv_x_high, inv_x_high, inv_x_low], axis=1)
+    fwd_y, inv_y = np.stack(split(fwd_y)), np.stack(split(inv_y))
+    return bf16(fwd_z), bf16(fwd_x), fwd_y, inv_y, inv_x, bf16(inv_z)
 
 
 def gelu_slope(values):
@@ -75,16 +83,31 @@
     return jnp.dot(left, right, preferred_element_type=F32)
 
 
+def halves(value):
+    high = value.astype(BF16)
+    return high, (value - high.astype(F32)).astype(BF16)
+
+
+def product(left, right, contracted):
+    def one(first, second):
+        return lax.dot_general(
+            first, second, ((contracted[:1], contracted[1:]), ((), ())), preferred_element_type=F32
+        )
+
+    return one(left[0], right[0]) + (one(left[1], right[0]) + one(left[0], right[1]))
+
+
 def lanes(blocks):
     return jnp.concatenate(blocks, axis=1)
 
 
-def to_modes(field, table_z, table_x, sent):
-    sections = []
-    for g in range(4):
-        along_z = dot(lanes([field[8 * g + j] for j in range(8)]), table_z[...])
-        both = jnp.concatenate([along_z[:, :N], along_z[:, N:]], axis=0).astype(BF16)
-        sections.append(dot(table_x[...], both))
+def section(field, g, table_z, table_x):
+    along_z = dot(lanes([field[8 * g + j] for j in range(8)]), table_z[...])
+    both = jnp.concatenate([along_z[:, :N], along_z[:, N:]], axis=0).astype(BF16)
+    return dot(table_x[...], both)
+
+
+def to_blocks(sections, sent):
     for q in range(4):
         sent[64 * q : 64 * q + 64, :] = lanes([v[:, 32 * q : 32 * q + 32] for v in sections])
 
@@ -99,11 +122,8 @@
 
 
 def along_y(received, table_y, rows, put):
-    both = lax.dot_general(
-        received[...].reshape(256, N).astype(BF16),
-        table_y[...],
-        (((0,), (0,)), ((), ())),
-        preferred_element_type=F32,
+    both = product(
+        halves(received[...].reshape(256, N)), (table_y[0], table_y[1]), (0, 0)
     )
     block = k4_lanes(32)
     for part in range(2):
@@ -125,15 +145,18 @@
     prod, prod_rows, kron, skip_rows, m_own, m_one, m_two_own, m_two, m_three_own, m_three,
     load_sem, out_sem, send_sem, recv_sem,
 ):
+    def group(ref, g):
+        return ref.at[8 * g : 8 * g + 8]
+
+    pairs = [(fz_hbm, fz)]
+    for g in range(4):
+        pairs += [(group(src, g), group(dst, g)) for src, dst in ((pre_hbm, v_pre), (cot_hbm, v_cot))]
+    pairs += [
+        (fx_hbm, fx), (in_hbm, v_in), (skip_hbm, v_skip), (fy_hbm, fy), (weight_hbm, v_weight),
+        (iy_hbm, iy), (ix_hbm, ix), (iz_hbm, iz),
+    ]
     loads = [
-        pltpu.make_async_copy(src, dst, load_sem.at[n])
-        for n, (src, dst) in enumerate(
-            (
-                (in_hbm, v_in), (fz_hbm, fz), (fx_hbm, fx), (pre_hbm, v_pre), (cot_hbm, v_cot),
-                (skip_hbm, v_skip), (fy_hbm, fy), (weight_hbm, v_weight), (iy_hbm, iy),
-                (ix_hbm, ix), (iz_hbm, iz),
-            )
-        )
+        pltpu.make_async_copy(src, dst, load_sem.at[n]) for n, (src, dst) in enumerate(pairs)
     ]
     for copy in loads:
         copy.start()
@@ -150,22 +173,27 @@
         peer = (t + k) % 16
         return peer, peer // 2 % 2 * 64 + b * 8 + peer % 2 * 4 + peer // 4
 
+    def near_first():
+        z = place % 8
+        for step in (4, 3, 5, 2, 6, 1, 7, 0):
+            c = (z + step) % 8
+            for side in (1 - a, a):
+                if step or side is not a:
+                    yield c % 4 * 4 + side * 2 + c // 4, side * 64 + b * 8 + c
+
     def far(k):
         peer = (b + k) % 8
         return peer, a * 64 + peer * 8 + h * 4 + q
 
+    def far_first():
+        return [far(k) for k in (4, 3, 5, 2, 6, 1, 7)]
+
     def other(k):
         return (sample + k) % BATCH
 
     barrier = pltpu.get_barrier_semaphore()
-
-    @pl.loop(1, 16)
-    def _(k):
-        pl.semaphore_signal(barrier, inc=1, device_id={"space": near(k)[1]}, device_id_type=MESH)
-
-    @pl.loop(1, 8)
-    def _(k):
-        pl.semaphore_signal(barrier, inc=1, device_id={"space": far(k)[1]}, device_id_type=MESH)
+    for _, where in [*near_first(), *far_first()]:
+        pl.semaphore_signal(barrier, inc=1, device_id={"space": where}, device_id_type=MESH)
 
     @pl.loop(1, BATCH)
     def _(k):
@@ -181,20 +209,14 @@
         return ref.at[pl.ds(pl.multiple_of(slot * 16, 16), 16), :]
 
     def send_near(src, dst, n):
+        for peer, where in near_first():
+            remote(rows16(src, peer), rows16(dst, t), n, {"space": where}).start()
         pltpu.make_async_copy(rows16(src, t), rows16(dst, t), recv_sem.at[n]).start()
 
-        @pl.loop(1, 16)
-        def _(k):
-            peer, where = near(k)
-            remote(rows16(src, peer), rows16(dst, t), n, {"space": where}).start()
-
     def send_far(src, dst, n):
+        for peer, where in far_first():
+            remote(src.at[peer], dst.at[b], n, {"space": where}).start()
         pltpu.make_async_copy(src.at[b], dst.at[b], recv_sem.at[n]).start()
-
-        @pl.loop(1, 8)
-        def _(k):
-            peer, where = far(k)
-            remote(src.at[peer], dst.at[b], n, {"space": where}).start()
 
     def send_batch(src, dst, n):
         pltpu.make_async_copy(src, dst.at[sample], recv_sem.at[n]).start()
@@ -209,27 +231,25 @@
     def left(ref, n):
         pltpu.make_async_copy(ref, ref, send_sem.at[n]).wait()
 
-    for n in range(3):
-        loads[n].wait()
-    to_modes(v_in, fz, fx, u_send)
+    loads[0].wait()
+    sections = []
+    for g in range(4):
+        loads[1 + 2 * g].wait()
+        loads[2 + 2 * g].wait()
+        for c in range(8 * g, 8 * g + 8):
+            slope = gelu_slope(v_pre[c].astype(F32))
+            v_cp[c] = (v_cot[c].astype(F32) * slope).astype(BF16)
+        if g == 0:
+            loads[9].wait()
+        sections.append(section(v_cp, g, fz, fx))
+    to_blocks(sections, e_send)
     pl.semaphore_wait(barrier, 15 + 7 + BATCH - 1)
+    send_near(e_send, e_mid, 1)
+
+    loads[10].wait()
+    to_blocks([section(v_in, g, fz, fx) for g in range(4)], u_send)
     send_near(u_send, u_mid, 0)
 
-    loads[3].wait()
-    loads[4].wait()
-
-    @pl.loop(0, CHANNELS)
-    def _(c):
-        slope = gelu_slope(v_pre[c].astype(F32))
-        v_cp[c] = (v_cot[c].astype(F32) * slope).astype(BF16)
-
-    to_modes(v_cp, fz, fx, e_send)
-    send_near(e_send, e_mid, 1)
-    arrived(u_mid, 0)
-    turn(u_mid, u_turn)
-    send_far(u_turn, u_all, 2)
-
-    loads[5].wait()
     chunks = range(8)
     prod[...] = lax.dot_general(
         lanes([v_in[:, 16 * j : 16 * j + 16, :].reshape(512, N) for j in chunks]),
@@ -268,7 +288,11 @@
     arrived(e_mid, 1)
     turn(e_mid, e_turn)
     send_far(e_turn, e_all, 4)
-
+    arrived(u_mid, 0)
+    turn(u_mid, u_turn)
+    send_far(u_turn, u_all, 2)
+
+    loads[11].wait()
     tall = lax.broadcasted_iota(jnp.int32, (32, 512), 1) // 16
     spread_t = tall == lax.broadcasted_iota(jnp.int32, (32, 512), 0)
     repeated = dot(v_skip[...], spread_t.astype(F32).astype(BF16))
@@ -285,16 +309,8 @@
                 32, 16, N
             )
 
-    arrived(u_all, 2)
-    loads[6].wait()
-
-    def put_u(part, value):
-        u_own[32 * part : 32 * part + 32, :] = value
-
-    along_y(u_all, fy, rows, put_u)
-    send_batch(u_own, u_batch, 5)
-
     arrived(e_all, 4)
+    loads[12].wait()
     e_rounded = []
 
     def put_e(part, value):
@@ -304,7 +320,7 @@
 
     along_y(e_all, fy, rows, put_e)
 
-    loads[7].wait()
+    loads[13].wait()
     e_real, e_imag = e_rounded
     for i in range(CHANNELS):
         w_real = v_weight[0, i].astype(F32)
@@ -326,13 +342,9 @@
         value = value * scale
         for k4 in range(4):
             back_rows[part, pl.ds(k4, 32, stride=4), :] = jnp.where(block == k4, value, 0.0)
-    loads[8].wait()
-    g_send[...] = lax.dot_general(
-        iy[...],
-        lanes([back_rows[0], back_rows[1]]).astype(BF16),
-        (((1,), (1,)), ((), ())),
-        preferred_element_type=F32,
-    )
+    loads[14].wait()
+    back = halves(lanes([back_rows[0], back_rows[1]]))
+    g_send[...] = product((iy[0], iy[1]), back, (1, 1))
     send_near(g_send, g_mid, 6)
 
     pltpu.make_async_copy(e_own.at[sample], e_batch.at[sample], recv_sem.at[7]).start()
@@ -341,6 +353,14 @@
     def _(k):
         peer = other(k)
         remote(e_own.at[peer], e_batch.at[sample], 7, {"batch": peer}).start()
+
+    arrived(u_all, 2)
+
+    def put_u(part, value):
+        u_own[32 * part : 32 * part + 32, :] = value
+
+    along_y(u_all, fy, rows, put_u)
+    send_batch(u_own, u_batch, 5)
 
     arrived(m_one, 3)
     total = m_one[0]
@@ -381,8 +401,8 @@
     m_three_own[...] = total
     send_batch(m_three_own, m_three, 10)
 
-    loads[9].wait()
-    loads[10].wait()
+    loads[15].wait()
+    loads[16].wait()
     arrived(g_all, 9)
     outs = []
     for g in range(4):
@@ -392,7 +412,8 @@
                 for n in range(4)
             ]
         )
-        along_x = dot(ix[...], spectra.astype(BF16))
+        high, low = halves(spectra)
+        along_x = dot(ix[...], jnp.concatenate([high, low, high], axis=0))
         both = lanes([along_x[:N], along_x[N:]]).astype(BF16)
         for n in range(4):
             grid = dot(both, iz[:, 256 * n : 256 * n + 256])
@@ -461,11 +482,11 @@
             pltpu.VMEM((8, N), F32), pltpu.VMEM((16, 8, N), F32),
             pltpu.VMEM((8, N), F32), pltpu.VMEM((8, 8, N), F32),
             pltpu.VMEM((8, N), F32), pltpu.VMEM((BATCH, 8, N), F32),
-            pltpu.SemaphoreType.DMA((11,)), pltpu.SemaphoreType.DMA((6,)),
+            pltpu.SemaphoreType.DMA((17,)), pltpu.SemaphoreType.DMA((6,)),
             pltpu.SemaphoreType.DMA((11,)), pltpu.SemaphoreType.DMA((11,)),
         ],
         compiler_params=pltpu.CompilerParams(
-            collective_id=0, has_side_effects=True, vmem_limit_bytes=48 * 2**20
+            collective_id=0, has_side_effects=True, vmem_limit_bytes=62 * 2**20
         ),
     )(
         inputs.reshape(field), pre_act.reshape(field), cotangent.reshape(field),

time: 56.3 us -> 44.3 us (0.79); the launches traced: 55.4 us -> 44.1 us
  local copies, waits for them, and re-layouts: 11.9 us -> 3.67 us
  Pallas kernels: 42.8 us -> 39.8 us
    unnamed x23 -> x7, local copies, waits for them, and re-layouts: 11.9 us -> 3.67 us
    pallas_call x1, Pallas kernels: 42.8 us -> 39.8 us  [on_device(): pl.pallas_call(kernel, out_shape=(jax.ShapeDtypeStruct(field, BF16), jax....]
where the time goes in v2:
time: 44.3 us; the launch traced here: 44.1 us
  Pallas kernels  39.8 us (90%)
  local copies, waits for them, and re-layouts  3.67 us (8%)
  between operations  0.65 us (1%)
    pallas_call x1, Pallas kernels, on_device(): pl.pallas_call(kernel, out_shape=(jax.ShapeDtypeStruct(field, BF16), jax....  39.8 us
    unnamed x7, local copies, waits for them, and re-layouts  3.67 us

profile of v2, /device:TPU:1, one launch (start us, length us, event | category | flops | bytes accessed | tf_op | source)
XLA Modules:
  0.0 44.1 jit_solution(2225545117156385908)
XLA Ops:
  0.6 39.8 %shard_map.130 = (bf16[32,128,128]{2,1,0:T(8,128)(2,1)}, f32[2,32,8,128]{3,2,1,0:T(8,128)}, f32[32,32]{1,0:T(8,128)}) custom-call(bf16[32,128,128]{2,1,0:T(8,128)(2,1)} %bitcast.7, bf16[32,128,128]{2,1,0:T(8,128)(2,1)} %bitcast.8, bf16[32,128,128]{2,1,0:T(8,128)(2,1)} %bitcast.9, bf16[2,32,32,128]{3,2,1,0:T(8,128)(2,1)} %weight_hbm.1, ...), custom_call_target="tpu_custom_call" | custom-call | tf_op jit(solution)/shard_map/pallas_call | solution.py:461
  40.4 0.0 copy-start
  40.4 2.3 %copy.18 = bf16[1,32,128,1,128]{4,2,3,1,0:T(8,128)(2,1)} copy(bf16[1,32,128,1,128]{4,2,3,1,0:T(8,128)(2,1)} %bitcast.6) | data formatting | bytes 2097152
  42.8 0.0 copy-done
  42.8 0.0 copy-start.1
  42.8 0.7 %copy.19 = f32[2,32,8,128]{3,2,1,0:T(8,128)} copy(f32[2,32,8,128]{3,2,1,0:T(8,128)S(1)} %copy-done) | data formatting | bytes 524288
  43.5 0.0 copy-done.1
  43.5 0.6 %copy.20 = f32[32,32]{1,0:T(8,128)} copy(f32[32,32]{1,0:T(8,128)S(1)} %copy-done.1) | data formatting | bytes 8192
Async XLA Ops:
  40.4 2.4 %copy-start = (f32[2,32,8,128]{3,2,1,0:T(8,128)S(1)}, f32[2,32,8,128]{3,2,1,0:T(8,128)}, u32[]{:S(2)}) copy-start(f32[2,32,8,128]{3,2,1,0:T(8,128)} %get-tuple-element.16) | copy-start | bytes 786436
  42.8 0.7 %copy-start.1 = (f32[32,32]{1,0:T(8,128)S(1)}, f32[32,32]{1,0:T(8,128)}, u32[]{:S(2)}) copy-start(f32[32,32]{1,0:T(8,128)} %get-tuple-element.17) | copy-start | bytes 12292

commit v3 on v2

--- a/solution.py
+++ b/solution.py
@@ -134,16 +134,16 @@
         put(part, value)
 
 
-def kernel(
+def spectral_kernel(
     in_hbm, pre_hbm, cot_hbm, weight_hbm, skip_hbm,
     fz_hbm, fx_hbm, fy_hbm, iy_hbm, ix_hbm, iz_hbm,
-    out_hbm, spectral_hbm, mixgrad_hbm,
-    v_in, v_pre, v_cot, v_weight, v_skip, fz, fx, fy, iy, ix, iz,
-    v_cp, v_mix, v_out, v_spectral, v_mixgrad,
+    v_grid, v_mix, ix, iz, v_spectral, v_mixgrad,
+    v_in, v_pre, v_cot, v_weight, v_skip, fz, fx, fy, iy,
+    v_cp,
     u_send, u_mid, u_turn, u_all, e_send, e_mid, e_turn, e_all, g_send, g_mid, g_turn, g_all,
     u_own, u_batch, e_own, e_batch, rows, partial, back_rows,
     prod, prod_rows, kron, skip_rows, m_own, m_one, m_two_own, m_two, m_three_own, m_three,
-    load_sem, out_sem, send_sem, recv_sem,
+    load_sem, send_sem, recv_sem,
 ):
     def group(ref, g):
         return ref.at[8 * g : 8 * g + 8]
@@ -391,8 +391,6 @@
             imag = imag + (u_real * e_i - u_imag * e_r)
         v_spectral[0, i] = real * scale
         v_spectral[1, i] = imag * scale
-    spectral_copy = pltpu.make_async_copy(v_spectral, spectral_hbm, out_sem.at[4])
-    spectral_copy.start()
 
     arrived(m_two, 8)
     total = m_two[0]
@@ -401,14 +399,41 @@
     m_three_own[...] = total
     send_batch(m_three_own, m_three, 10)
 
+    arrived(m_three, 10)
+    total = (m_three[0] + m_three[1] + (m_three[2] + m_three[3])) / math.sqrt(BATCH * N * N * N)
+    for r in range(4):
+        v_mixgrad[8 * r : 8 * r + 8, :] = total[:, 32 * r : 32 * r + 32]
+
     loads[15].wait()
     loads[16].wait()
     arrived(g_all, 9)
-    outs = []
+    v_grid[...] = g_all[...]
+
+    left(u_send.at[0:240], 0)
+    left(e_send.at[0:240], 1)
+    left(u_turn.at[0:7], 2)
+    left(m_one.at[0:15], 3)
+    left(e_turn.at[0:7], 4)
+    left(u_batch.at[0:3], 5)
+    left(g_send.at[0:240], 6)
+    left(e_own.at[0:3], 7)
+    left(m_two.at[0:7], 8)
+    left(g_turn.at[0:7], 9)
+    left(m_three.at[0:3], 10)
+
+def grid_kernel(
+    v_grid, v_mix, ix, iz, v_spectral, v_mixgrad, out_hbm, spectral_hbm, mixgrad_hbm, v_out, sems
+):
+    copies = [
+        pltpu.make_async_copy(v_spectral, spectral_hbm, sems.at[4]),
+        pltpu.make_async_copy(v_mixgrad, mixgrad_hbm, sems.at[5]),
+    ]
+    for copy in copies:
+        copy.start()
     for g in range(4):
         spectra = lanes(
             [
-                g_all[:, 8 * n : 8 * n + 8, 32 * g : 32 * g + 32].reshape(64, 32)
+                v_grid[:, 8 * n : 8 * n + 8, 32 * g : 32 * g + 32].reshape(64, 32)
                 for n in range(4)
             ]
         )
@@ -421,33 +446,12 @@
                 i = 8 * g + 2 * n + r
                 v_out[i] = (grid[:, N * r : N * r + N] + v_mix[i]).astype(BF16)
         copy = pltpu.make_async_copy(
-            v_out.at[8 * g : 8 * g + 8], out_hbm.at[8 * g : 8 * g + 8], out_sem.at[g]
+            v_out.at[8 * g : 8 * g + 8], out_hbm.at[8 * g : 8 * g + 8], sems.at[g]
         )
         copy.start()
-        outs.append(copy)
-
-    arrived(m_three, 10)
-    total = (m_three[0] + m_three[1] + (m_three[2] + m_three[3])) / math.sqrt(BATCH * N * N * N)
-    for r in range(4):
-        v_mixgrad[8 * r : 8 * r + 8, :] = total[:, 32 * r : 32 * r + 32]
-    mixgrad_copy = pltpu.make_async_copy(v_mixgrad, mixgrad_hbm, out_sem.at[5])
-    mixgrad_copy.start()
-
-    left(u_send.at[0:240], 0)
-    left(e_send.at[0:240], 1)
-    left(u_turn.at[0:7], 2)
-    left(m_one.at[0:15], 3)
-    left(e_turn.at[0:7], 4)
-    left(u_batch.at[0:3], 5)
-    left(g_send.at[0:240], 6)
-    left(e_own.at[0:3], 7)
-    left(m_two.at[0:7], 8)
-    left(g_turn.at[0:7], 9)
-    left(m_three.at[0:3], 10)
-    for copy in outs:
+        copies.append(copy)
+    for copy in copies:
         copy.wait()
-    spectral_copy.wait()
-    mixgrad_copy.wait()
 
 
 def on_device(inputs, pre_act, cotangent, spectral_weight, skip_weight):
@@ -458,21 +462,30 @@
         pltpu.VMEM((8, 32, N), F32), pltpu.VMEM((8, 32, N), F32),
     ]
     anywhere = pl.BlockSpec(memory_space=pl.ANY)
-    grad_inputs, grad_spectral, grad_skip = pl.pallas_call(
-        kernel,
+    near = pl.BlockSpec(memory_space=pltpu.VMEM)
+    spectral_type = jax.ShapeDtypeStruct((2, CHANNELS, 8, N), F32)
+    skip_type = jax.ShapeDtypeStruct((CHANNELS, CHANNELS), F32)
+    operands = [
+        inputs.reshape(field), pre_act.reshape(field), cotangent.reshape(field),
+        spectral_weight, skip_weight, *tables,
+    ]
+    stages = pl.pallas_call(
+        spectral_kernel,
         out_shape=(
-            jax.ShapeDtypeStruct(field, BF16),
-            jax.ShapeDtypeStruct((2, CHANNELS, 8, N), F32),
-            jax.ShapeDtypeStruct((CHANNELS, CHANNELS), F32),
+            jax.ShapeDtypeStruct((8, 32, N), F32),
+            jax.ShapeDtypeStruct(field, F32),
+            jax.ShapeDtypeStruct(tables[4].shape, BF16),
+            jax.ShapeDtypeStruct(tables[5].shape, BF16),
+            spectral_type,
+            skip_type,
         ),
         in_specs=[anywhere] * 11,
-        out_specs=(anywhere,) * 3,
+        out_specs=(near,) * 6,
         scratch_shapes=[
             pltpu.VMEM(field, BF16), pltpu.VMEM(field, BF16), pltpu.VMEM(field, BF16),
             pltpu.VMEM((2, 32, 32, N), BF16), pltpu.VMEM((32, 32), BF16),
-            *(pltpu.VMEM(v.shape, BF16) for v in tables),
-            pltpu.VMEM(field, BF16), pltpu.VMEM(field, F32), pltpu.VMEM(field, BF16),
-            pltpu.VMEM((2, 32, 8, N), F32), pltpu.VMEM((32, 32), F32),
+            *(pltpu.VMEM(v.shape, BF16) for v in tables[:4]),
+            pltpu.VMEM(field, BF16),
             *exchange, *exchange, *exchange,
             pltpu.VMEM((64, N), F32), pltpu.VMEM((BATCH, 64, N), F32),
             pltpu.VMEM((4, 16, N), F32), pltpu.VMEM((BATCH, 16, N), F32),
@@ -482,16 +495,21 @@
             pltpu.VMEM((8, N), F32), pltpu.VMEM((16, 8, N), F32),
             pltpu.VMEM((8, N), F32), pltpu.VMEM((8, 8, N), F32),
             pltpu.VMEM((8, N), F32), pltpu.VMEM((BATCH, 8, N), F32),
-            pltpu.SemaphoreType.DMA((17,)), pltpu.SemaphoreType.DMA((6,)),
+            pltpu.SemaphoreType.DMA((17,)),
             pltpu.SemaphoreType.DMA((11,)), pltpu.SemaphoreType.DMA((11,)),
         ],
         compiler_params=pltpu.CompilerParams(
-            collective_id=0, has_side_effects=True, vmem_limit_bytes=62 * 2**20
+            collective_id=0, has_side_effects=True, vmem_limit_bytes=40 * 2**20
         ),
-    )(
-        inputs.reshape(field), pre_act.reshape(field), cotangent.reshape(field),
-        spectral_weight, skip_weight, *tables,
-    )
+    )(*(pltpu.with_memory_space_constraint(v, pltpu.HBM) for v in operands))
+    grad_inputs, grad_spectral, grad_skip = pl.pallas_call(
+        grid_kernel,
+        out_shape=(jax.ShapeDtypeStruct(field, BF16), spectral_type, skip_type),
+        in_specs=[near] * 6,
+        out_specs=(anywhere,) * 3,
+        scratch_shapes=[pltpu.VMEM(field, BF16), pltpu.SemaphoreType.DMA((6,))],
+        compiler_params=pltpu.CompilerParams(vmem_limit_bytes=24 * 2**20),
+    )(*stages)
     return grad_inputs.reshape(inputs.shape), grad_spectral, grad_skip
 
 

time: 44.3 us -> 41.8 us (0.944)
  local copies, waits for them, and re-layouts: 3.67 us -> 0 us
  Pallas kernels: 39.8 us -> 41 us
    unnamed x7 -> x0, local copies, waits for them, and re-layouts: 3.67 us -> none
    pallas_call x1 -> x2, Pallas kernels: 39.8 us -> 41 us  [the longest x1 39.1 us: on_device(): pl.pallas_call(spectral_kernel, out_shape=(jax.ShapeDtypeStruct((8, 32, N...]
where the time goes in v3:
time: 41.8 us; the launch traced here: 41.7 us
  Pallas kernels  41 us (98%)
  between operations  0.64 us (2%)
    pallas_call x1, Pallas kernels, on_device(): pl.pallas_call(spectral_kernel, out_shape=(jax.ShapeDtypeStruct((8, 32, N...  39.1 us
    pallas_call x1, Pallas kernels, on_device(): pl.pallas_call(grid_kernel, out_shape=(jax.ShapeDtypeStruct(field, BF16),...  1.9 us

profile of v3, /device:TPU:1, one launch (start us, length us, event | category | flops | bytes accessed | tf_op | source)
XLA Modules:
  0.0 41.7 jit_solution(15465164905036500953)
XLA Ops:
  0.6 39.1 %shard_map.130 = (f32[8,32,128]{2,1,0:T(8,128)S(1)}, f32[32,128,128]{2,1,0:T(8,128)S(1)}, bf16[256,192]{1,0:T(8,128)(2,1)S(1)}, bf16[256,1024]{1,0:T(8,128)(2,1)...) custom-call(bf16[32,128,128]{2,1,0:T(8,128)(2,1)} %bitcast.6, bf16[32,128,128]{2,1,0:T(8,128)(2,1)} %bitcast.7, ...), custom_call_target="tpu_custom_call" | custom-call | tf_op jit(solution)/shard_map/pallas_call | solution.py:472
  39.8 1.9 %shard_map.131 = (bf16[32,128,128]{2,1,0:T(8,128)(2,1)}, f32[2,32,8,128]{3,2,1,0:T(8,128)}, f32[32,32]{1,0:T(8,128)}) custom-call(f32[8,32,128]{2,1,0:T(8,128)S(1)} %get-tuple-element.12.v_grid, f32[32,128,128]{2,1,0:T(8,128)S(1)} %get-tuple-element.13.v_mix, bf16[256,192]{1,0:T(8,128)(2,1)S(1)} %get-tuple-element.14.ix, ...), custom_call_target="tpu_custom_call" | custom-call | tf_op jit(solution)/shard_map/pallas_call | solution.py:505

commit v4 on v3

--- a/solution.py
+++ b/solution.py
@@ -55,8 +55,8 @@
     parts = parts.reshape(2, 2, N, 2, 8, 2)
     fwd_x = np.transpose(parts, (3, 5, 0, 4, 1, 2)).reshape(64, 256)
     cos_x, sin_x = phases(points, signed(np.arange(32)))
-    parts = np.stack([np.stack([cos_x, -sin_x]), np.stack([sin_x, cos_x])]).reshape(2, 2, N, 2, 8, 2)
-    inv_x = np.transpose(parts, (0, 2, 4, 3, 5, 1)).reshape(256, 64)
+    parts = np.stack([np.stack([cos_x, -sin_x]), np.stack([sin_x, cos_x])])
+    inv_x = np.transpose(parts, (0, 2, 3, 1)).reshape(256, 64)
     q, a, h = places()
     y = a[None, :] * 64 + np.arange(8)[:, None] * 8 + h[None, :] * 4 + q[None, :]
     cos_y, sin_y = phases(y.reshape(-1), signed(np.arange(32)))
@@ -64,9 +64,10 @@
     parts = np.stack([np.stack([cos_y, sin_y]), np.stack([-sin_y, cos_y])])
     fwd_y = np.transpose(parts, (2, 3, 1, 0, 4))[:, :, :, :, None, :]
     fwd_y = np.broadcast_to(fwd_y, (8, 16, 2, 2, 4, 32)).reshape(256, 256)
+    cos_y, sin_y = phases(points, signed(np.arange(32)))
     parts = np.stack([np.stack([cos_y, -sin_y]), np.stack([sin_y, cos_y])])
-    inv_y = np.transpose(parts, (3, 0, 2, 1, 4))[:, :, :, :, None, :]
-    inv_y = np.broadcast_to(inv_y, (16, 2, 8, 2, 4, 32)).reshape(256, 256)
+    inv_y = np.transpose(parts, (2, 0, 1, 3))[:, :, :, None, :]
+    inv_y = np.broadcast_to(inv_y, (N, 2, 2, 4, 32)).reshape(256, 256)
     inv_x_high, inv_x_low = split(inv_x)
     inv_x = np.concatenate([inv_x_high, inv_x_high, inv_x_low], axis=1)
     fwd_y, inv_y = np.stack(split(fwd_y)), np.stack(split(inv_y))
@@ -101,10 +102,20 @@
     return jnp.concatenate(blocks, axis=1)
 
 
-def section(field, g, table_z, table_x):
-    along_z = dot(lanes([field[8 * g + j] for j in range(8)]), table_z[...])
-    both = jnp.concatenate([along_z[:, :N], along_z[:, N:]], axis=0).astype(BF16)
-    return dot(table_x[...], both)
+def all_sections(field, table_z, table_x):
+    planes = [
+        jnp.concatenate([field[8 * g + j] for g in range(4)], axis=0) for j in range(8)
+    ]
+    along_z = dot(lanes(planes), table_z[...])
+    both = jnp.concatenate(
+        [
+            lanes([along_z[N * g : N * g + N, N * part : N * part + N] for g in range(4)])
+            for part in range(2)
+        ],
+        axis=0,
+    ).astype(BF16)
+    found = dot(table_x[...], both)
+    return [found[:, N * g : N * g + N] for g in range(4)]
 
 
 def to_blocks(sections, sent):
@@ -140,27 +151,11 @@
     v_grid, v_mix, ix, iz, v_spectral, v_mixgrad,
     v_in, v_pre, v_cot, v_weight, v_skip, fz, fx, fy, iy,
     v_cp,
-    u_send, u_mid, u_turn, u_all, e_send, e_mid, e_turn, e_all, g_send, g_mid, g_turn, g_all,
+    u_send, u_mid, u_turn, u_all, e_send, e_mid, e_turn, e_all, g_send, g_all,
     u_own, u_batch, e_own, e_batch, rows, partial, back_rows,
     prod, prod_rows, kron, skip_rows, m_own, m_one, m_two_own, m_two, m_three_own, m_three,
     load_sem, send_sem, recv_sem,
 ):
-    def group(ref, g):
-        return ref.at[8 * g : 8 * g + 8]
-
-    pairs = [(fz_hbm, fz)]
-    for g in range(4):
-        pairs += [(group(src, g), group(dst, g)) for src, dst in ((pre_hbm, v_pre), (cot_hbm, v_cot))]
-    pairs += [
-        (fx_hbm, fx), (in_hbm, v_in), (skip_hbm, v_skip), (fy_hbm, fy), (weight_hbm, v_weight),
-        (iy_hbm, iy), (ix_hbm, ix), (iz_hbm, iz),
-    ]
-    loads = [
-        pltpu.make_async_copy(src, dst, load_sem.at[n]) for n, (src, dst) in enumerate(pairs)
-    ]
-    for copy in loads:
-        copy.start()
-
     sample = lax.axis_index("batch")
     place = lax.axis_index("space")
     a = place // 64
@@ -199,6 +194,22 @@
     def _(k):
         pl.semaphore_signal(barrier, inc=1, device_id={"batch": other(k)}, device_id_type=MESH)
 
+    def group(ref, g):
+        return ref.at[8 * g : 8 * g + 8]
+
+    pairs = []
+    for g in range(4):
+        pairs += [(group(src, g), group(dst, g)) for src, dst in ((pre_hbm, v_pre), (cot_hbm, v_cot))]
+    pairs += [
+        (fz_hbm, fz), (fx_hbm, fx), (in_hbm, v_in), (skip_hbm, v_skip), (fy_hbm, fy), (weight_hbm, v_weight),
+        (iy_hbm, iy), (ix_hbm, ix), (iz_hbm, iz),
+    ]
+    loads = [
+        pltpu.make_async_copy(src, dst, load_sem.at[n]) for n, (src, dst) in enumerate(pairs)
+    ]
+    for copy in loads[:10]:
+        copy.start()
+
     def remote(src, dst, n, where):
         return pltpu.make_async_remote_copy(
             src_ref=src, dst_ref=dst, send_sem=send_sem.at[n], recv_sem=recv_sem.at[n],
@@ -218,6 +229,23 @@
             remote(src.at[peer], dst.at[b], n, {"space": where}).start()
         pltpu.make_async_copy(src.at[b], dst.at[b], recv_sem.at[n]).start()
 
+    def distant_first(index):
+        return 4 + (index + 1) // 2 * (1 - 2 * (index % 2))
+
+    def send_all(src, dst, n):
+        mine = dst.at[pl.ds(pl.multiple_of(64 * q + place // 4 * 2, 2), 2), :]
+
+        @pl.loop(0, N - 1)
+        def _(k):
+            y = (b + distant_first(k // 16)) % 8
+            z = (place + distant_first(k // 2 % 8)) % 8
+            where = (a + 1 + k % 2) % 2 * 64 + y * 8 + z
+            rows = src.at[pl.ds(pl.multiple_of(where * 2, 2), 2), :]
+            remote(rows, mine, n, {"space": where}).start()
+
+        rows = src.at[pl.ds(pl.multiple_of(place * 2, 2), 2), :]
+        pltpu.make_async_copy(rows, mine, recv_sem.at[n]).start()
+
     def send_batch(src, dst, n):
         pltpu.make_async_copy(src, dst.at[sample], recv_sem.at[n]).start()
 
@@ -231,23 +259,23 @@
     def left(ref, n):
         pltpu.make_async_copy(ref, ref, send_sem.at[n]).wait()
 
-    loads[0].wait()
-    sections = []
     for g in range(4):
-        loads[1 + 2 * g].wait()
-        loads[2 + 2 * g].wait()
+        loads[2 * g].wait()
+        loads[2 * g + 1].wait()
         for c in range(8 * g, 8 * g + 8):
             slope = gelu_slope(v_pre[c].astype(F32))
             v_cp[c] = (v_cot[c].astype(F32) * slope).astype(BF16)
-        if g == 0:
-            loads[9].wait()
-        sections.append(section(v_cp, g, fz, fx))
+    for copy in loads[10:]:
+        copy.start()
+    loads[8].wait()
+    loads[9].wait()
+    sections = all_sections(v_cp, fz, fx)
     to_blocks(sections, e_send)
     pl.semaphore_wait(barrier, 15 + 7 + BATCH - 1)
     send_near(e_send, e_mid, 1)
 
     loads[10].wait()
-    to_blocks([section(v_in, g, fz, fx) for g in range(4)], u_send)
+    to_blocks(all_sections(v_in, fz, fx), u_send)
     send_near(u_send, u_mid, 0)
 
     chunks = range(8)
@@ -309,6 +337,17 @@
                 32, 16, N
             )
 
+    arrived(m_one, 3)
+    total = m_one[0]
+    for n in range(1, 16):
+        total = total + m_one[n]
+    m_two_own[...] = total
+    pltpu.make_async_copy(m_two_own, m_two.at[b], recv_sem.at[8]).start()
+
+    @pl.loop(1, 8)
+    def _(k):
+        remote(m_two_own, m_two.at[b], 8, {"space": far(k)[1]}).start()
+
     arrived(e_all, 4)
     loads[12].wait()
     e_rounded = []
@@ -345,7 +384,7 @@
     loads[14].wait()
     back = halves(lanes([back_rows[0], back_rows[1]]))
     g_send[...] = product((iy[0], iy[1]), back, (1, 1))
-    send_near(g_send, g_mid, 6)
+    send_all(g_send, g_all, 9)
 
     pltpu.make_async_copy(e_own.at[sample], e_batch.at[sample], recv_sem.at[7]).start()
 
@@ -362,20 +401,12 @@
     along_y(u_all, fy, rows, put_u)
     send_batch(u_own, u_batch, 5)
 
-    arrived(m_one, 3)
-    total = m_one[0]
-    for n in range(1, 16):
-        total = total + m_one[n]
-    m_two_own[...] = total
-    pltpu.make_async_copy(m_two_own, m_two.at[b], recv_sem.at[8]).start()
-
-    @pl.loop(1, 8)
-    def _(k):
-        remote(m_two_own, m_two.at[b], 8, {"space": far(k)[1]}).start()
-
-    arrived(g_mid, 6)
-    turn(g_mid, g_turn)
-    send_far(g_turn, g_all, 9)
+    arrived(m_two, 8)
+    total = m_two[0]
+    for n in range(1, 8):
+        total = total + m_two[n]
+    m_three_own[...] = total
+    send_batch(m_three_own, m_three, 10)
 
     arrived(u_batch, 5)
     arrived(e_batch, 7)
@@ -392,13 +423,6 @@
         v_spectral[0, i] = real * scale
         v_spectral[1, i] = imag * scale
 
-    arrived(m_two, 8)
-    total = m_two[0]
-    for n in range(1, 8):
-        total = total + m_two[n]
-    m_three_own[...] = total
-    send_batch(m_three_own, m_three, 10)
-
     arrived(m_three, 10)
     total = (m_three[0] + m_three[1] + (m_three[2] + m_three[3])) / math.sqrt(BATCH * N * N * N)
     for r in range(4):
@@ -415,10 +439,9 @@
     left(m_one.at[0:15], 3)
     left(e_turn.at[0:7], 4)
     left(u_batch.at[0:3], 5)
-    left(g_send.at[0:240], 6)
     left(e_own.at[0:3], 7)
     left(m_two.at[0:7], 8)
-    left(g_turn.at[0:7], 9)
+    left(g_send.at[0:254], 9)
     left(m_three.at[0:3], 10)
 
 def grid_kernel(
@@ -430,23 +453,22 @@
     ]
     for copy in copies:
         copy.start()
+    stacked = []
     for g in range(4):
-        spectra = lanes(
-            [
-                v_grid[:, 8 * n : 8 * n + 8, 32 * g : 32 * g + 32].reshape(64, 32)
-                for n in range(4)
-            ]
-        )
+        spectra = lanes([v_grid[64 * n : 64 * n + 64, 32 * g : 32 * g + 32] for n in range(4)])
         high, low = halves(spectra)
         along_x = dot(ix[...], jnp.concatenate([high, low, high], axis=0))
-        both = lanes([along_x[:N], along_x[N:]]).astype(BF16)
-        for n in range(4):
-            grid = dot(both, iz[:, 256 * n : 256 * n + 256])
+        stacked.append(lanes([along_x[:N], along_x[N:]]).astype(BF16))
+    stacked = jnp.concatenate(stacked, axis=0)
+    for n in range(4):
+        grid = dot(stacked, iz[:, 256 * n : 256 * n + 256])
+        for g in range(4):
             for r in range(2):
                 i = 8 * g + 2 * n + r
-                v_out[i] = (grid[:, N * r : N * r + N] + v_mix[i]).astype(BF16)
+                block = grid[N * g : N * g + N, N * r : N * r + N]
+                v_out[g, 2 * n + r] = (block + v_mix[i]).astype(BF16)
         copy = pltpu.make_async_copy(
-            v_out.at[8 * g : 8 * g + 8], out_hbm.at[8 * g : 8 * g + 8], sems.at[g]
+            v_out.at[:, 2 * n : 2 * n + 2], out_hbm.at[:, 2 * n : 2 * n + 2], sems.at[n]
         )
         copy.start()
         copies.append(copy)
@@ -472,7 +494,7 @@
     stages = pl.pallas_call(
         spectral_kernel,
         out_shape=(
-            jax.ShapeDtypeStruct((8, 32, N), F32),
+            jax.ShapeDtypeStruct((256, N), F32),
             jax.ShapeDtypeStruct(field, F32),
             jax.ShapeDtypeStruct(tables[4].shape, BF16),
             jax.ShapeDtypeStruct(tables[5].shape, BF16),
@@ -486,7 +508,7 @@
             pltpu.VMEM((2, 32, 32, N), BF16), pltpu.VMEM((32, 32), BF16),
             *(pltpu.VMEM(v.shape, BF16) for v in tables[:4]),
             pltpu.VMEM(field, BF16),
-            *exchange, *exchange, *exchange,
+            *exchange, *exchange, pltpu.VMEM((256, N), F32), pltpu.VMEM((256, N), F32),
             pltpu.VMEM((64, N), F32), pltpu.VMEM((BATCH, 64, N), F32),
             pltpu.VMEM((4, 16, N), F32), pltpu.VMEM((BATCH, 16, N), F32),
             pltpu.VMEM((2, N, N), F32), pltpu.VMEM((2, 256, N), F32), pltpu.VMEM((2, N, N), F32),
@@ -504,10 +526,10 @@
     )(*(pltpu.with_memory_space_constraint(v, pltpu.HBM) for v in operands))
     grad_inputs, grad_spectral, grad_skip = pl.pallas_call(
         grid_kernel,
-        out_shape=(jax.ShapeDtypeStruct(field, BF16), spectral_type, skip_type),
+        out_shape=(jax.ShapeDtypeStruct((4, 8, N, N), BF16), spectral_type, skip_type),
         in_specs=[near] * 6,
         out_specs=(anywhere,) * 3,
-        scratch_shapes=[pltpu.VMEM(field, BF16), pltpu.SemaphoreType.DMA((6,))],
+        scratch_shapes=[pltpu.VMEM((4, 8, N, N), BF16), pltpu.SemaphoreType.DMA((6,))],
         compiler_params=pltpu.CompilerParams(vmem_limit_bytes=24 * 2**20),
     )(*stages)
     return grad_inputs.reshape(inputs.shape), grad_spectral, grad_skip

time: 41.8 us -> 42.5 us (1.017)
  Pallas kernels: 41 us -> 41.8 us
    pallas_call x2, Pallas kernels: 41 us -> 41.8 us  [the longest x1 40.2 us: on_device(): pl.pallas_call(spectral_kernel, out_shape=(jax.ShapeDtypeStruct((256, N),...]
where the time goes in v4:
time: 42.5 us; the launch traced here: 42.4 us
  Pallas kernels  41.8 us (98%)
  between operations  0.64 us (2%)
    pallas_call x1, Pallas kernels, on_device(): pl.pallas_call(spectral_kernel, out_shape=(jax.ShapeDtypeStruct((256, N),...  40.2 us
    pallas_call x1, Pallas kernels, on_device(): pl.pallas_call(grid_kernel, out_shape=(jax.ShapeDtypeStruct((4, 8, N, N),...  1.54 us

profile of v4, /device:TPU:1, one launch (start us, length us, event | category | flops | bytes accessed | tf_op | source)
XLA Modules:
  0.0 42.4 jit_solution(8826739690281789700)
XLA Ops:
  0.6 40.2 %shard_map.130 = (f32[256,128]{1,0:T(8,128)S(1)}, f32[32,128,128]{2,1,0:T(8,128)S(1)}, bf16[256,192]{1,0:T(8,128)(2,1)S(1)}, bf16[256,1024]{1,0:T(8,128)(2,1)S(1...) custom-call(bf16[32,128,128]{2,1,0:T(8,128)(2,1)} %bitcast.6, bf16[32,128,128]{2,1,0:T(8,128)(2,1)} %bitcast.7, ...), custom_call_target="tpu_custom_call" | custom-call | tf_op jit(solution)/shard_map/pallas_call | solution.py:494
  40.8 1.5 %shard_map.131 = (bf16[4,8,128,128]{3,2,1,0:T(8,128)(2,1)}, f32[2,32,8,128]{3,2,1,0:T(8,128)}, f32[32,32]{1,0:T(8,128)}) custom-call(f32[256,128]{1,0:T(8,128)S(1)} %get-tuple-element.12.v_grid, f32[32,128,128]{2,1,0:T(8,128)S(1)} %get-tuple-element.13.v_mix, bf16[256,192]{1,0:T(8,128)(2,1)S(1)} %get-tuple-element.14.ix, ...), custom_call_target="tpu_custom_call" | custom-call | tf_op jit(solution)/shard_map/pallas_call | solution.py:527

commit v5 on v4

--- a/solution.py
+++ b/solution.py
@@ -55,8 +55,8 @@
     parts = parts.reshape(2, 2, N, 2, 8, 2)
     fwd_x = np.transpose(parts, (3, 5, 0, 4, 1, 2)).reshape(64, 256)
     cos_x, sin_x = phases(points, signed(np.arange(32)))
-    parts = np.stack([np.stack([cos_x, -sin_x]), np.stack([sin_x, cos_x])])
-    inv_x = np.transpose(parts, (0, 2, 3, 1)).reshape(256, 64)
+    parts = np.stack([np.stack([cos_x, -sin_x]), np.stack([sin_x, cos_x])]).reshape(2, 2, N, 2, 8, 2)
+    inv_x = np.transpose(parts, (0, 2, 4, 3, 5, 1)).reshape(256, 64)
     q, a, h = places()
     y = a[None, :] * 64 + np.arange(8)[:, None] * 8 + h[None, :] * 4 + q[None, :]
     cos_y, sin_y = phases(y.reshape(-1), signed(np.arange(32)))
@@ -64,10 +64,9 @@
     parts = np.stack([np.stack([cos_y, sin_y]), np.stack([-sin_y, cos_y])])
     fwd_y = np.transpose(parts, (2, 3, 1, 0, 4))[:, :, :, :, None, :]
     fwd_y = np.broadcast_to(fwd_y, (8, 16, 2, 2, 4, 32)).reshape(256, 256)
-    cos_y, sin_y = phases(points, signed(np.arange(32)))
     parts = np.stack([np.stack([cos_y, -sin_y]), np.stack([sin_y, cos_y])])
-    inv_y = np.transpose(parts, (2, 0, 1, 3))[:, :, :, None, :]
-    inv_y = np.broadcast_to(inv_y, (N, 2, 2, 4, 32)).reshape(256, 256)
+    inv_y = np.transpose(parts, (3, 0, 2, 1, 4))[:, :, :, :, None, :]
+    inv_y = np.broadcast_to(inv_y, (16, 2, 8, 2, 4, 32)).reshape(256, 256)
     inv_x_high, inv_x_low = split(inv_x)
     inv_x = np.concatenate([inv_x_high, inv_x_high, inv_x_low], axis=1)
     fwd_y, inv_y = np.stack(split(fwd_y)), np.stack(split(inv_y))
@@ -128,13 +127,21 @@
         sent[b] = received[pl.ds(b, 32, stride=8), :]
 
 
+def cross(received, sent):
+    for t in range(16):
+        for part in range(2):
+            sent[16 * t + 8 * part : 16 * t + 8 * part + 8, :] = received[
+                pl.ds(2 * t + part, 8, stride=32), :
+            ]
+
+
 def k4_lanes(rows):
     return lax.broadcasted_iota(jnp.int32, (rows, N), 1) // 32
 
 
 def along_y(received, table_y, rows, put):
     both = product(
-        halves(received[...].reshape(256, N)), (table_y[0], table_y[1]), (0, 0)
+        halves(received[...]), (table_y[0], table_y[1]), (0, 0)
     )
     block = k4_lanes(32)
     for part in range(2):
@@ -151,7 +158,7 @@
     v_grid, v_mix, ix, iz, v_spectral, v_mixgrad,
     v_in, v_pre, v_cot, v_weight, v_skip, fz, fx, fy, iy,
     v_cp,
-    u_send, u_mid, u_turn, u_all, e_send, e_mid, e_turn, e_all, g_send, g_all,
+    u_send, u_mid, u_turn, u_all, u_near, u_last, e_send, e_mid, e_turn, e_all, g_send, g_mid, g_turn, g_all,
     u_own, u_batch, e_own, e_batch, rows, partial, back_rows,
     prod, prod_rows, kron, skip_rows, m_own, m_one, m_two_own, m_two, m_three_own, m_three,
     load_sem, send_sem, recv_sem,
@@ -225,26 +232,10 @@
         pltpu.make_async_copy(rows16(src, t), rows16(dst, t), recv_sem.at[n]).start()
 
     def send_far(src, dst, n):
+        mine = dst.at[pl.ds(pl.multiple_of(b * 32, 32), 32), :]
         for peer, where in far_first():
-            remote(src.at[peer], dst.at[b], n, {"space": where}).start()
-        pltpu.make_async_copy(src.at[b], dst.at[b], recv_sem.at[n]).start()
-
-    def distant_first(index):
-        return 4 + (index + 1) // 2 * (1 - 2 * (index % 2))
-
-    def send_all(src, dst, n):
-        mine = dst.at[pl.ds(pl.multiple_of(64 * q + place // 4 * 2, 2), 2), :]
-
-        @pl.loop(0, N - 1)
-        def _(k):
-            y = (b + distant_first(k // 16)) % 8
-            z = (place + distant_first(k // 2 % 8)) % 8
-            where = (a + 1 + k % 2) % 2 * 64 + y * 8 + z
-            rows = src.at[pl.ds(pl.multiple_of(where * 2, 2), 2), :]
-            remote(rows, mine, n, {"space": where}).start()
-
-        rows = src.at[pl.ds(pl.multiple_of(place * 2, 2), 2), :]
-        pltpu.make_async_copy(rows, mine, recv_sem.at[n]).start()
+            remote(src.at[peer], mine, n, {"space": where}).start()
+        pltpu.make_async_copy(src.at[b], mine, recv_sem.at[n]).start()
 
     def send_batch(src, dst, n):
         pltpu.make_async_copy(src, dst.at[sample], recv_sem.at[n]).start()
@@ -276,7 +267,8 @@
 
     loads[10].wait()
     to_blocks(all_sections(v_in, fz, fx), u_send)
-    send_near(u_send, u_mid, 0)
+    turn(u_send, u_turn)
+    send_far(u_turn, u_mid, 0)
 
     chunks = range(8)
     prod[...] = lax.dot_general(
@@ -317,8 +309,8 @@
     turn(e_mid, e_turn)
     send_far(e_turn, e_all, 4)
     arrived(u_mid, 0)
-    turn(u_mid, u_turn)
-    send_far(u_turn, u_all, 2)
+    cross(u_mid, u_near)
+    send_near(u_near, u_last, 2)
 
     loads[11].wait()
     tall = lax.broadcasted_iota(jnp.int32, (32, 512), 1) // 16
@@ -384,7 +376,7 @@
     loads[14].wait()
     back = halves(lanes([back_rows[0], back_rows[1]]))
     g_send[...] = product((iy[0], iy[1]), back, (1, 1))
-    send_all(g_send, g_all, 9)
+    send_near(g_send, g_mid, 6)
 
     pltpu.make_async_copy(e_own.at[sample], e_batch.at[sample], recv_sem.at[7]).start()
 
@@ -393,7 +385,9 @@
         peer = other(k)
         remote(e_own.at[peer], e_batch.at[sample], 7, {"batch": peer}).start()
 
-    arrived(u_all, 2)
+    arrived(u_last, 2)
+    for n in range(8):
+        u_all[32 * n : 32 * n + 32, :] = u_last[pl.ds(n, 32, stride=8), :]
 
     def put_u(part, value):
         u_own[32 * part : 32 * part + 32, :] = value
@@ -407,6 +401,10 @@
         total = total + m_two[n]
     m_three_own[...] = total
     send_batch(m_three_own, m_three, 10)
+
+    arrived(g_mid, 6)
+    turn(g_mid, g_turn)
+    send_far(g_turn, g_all, 9)
 
     arrived(u_batch, 5)
     arrived(e_batch, 7)
@@ -433,15 +431,16 @@
     arrived(g_all, 9)
     v_grid[...] = g_all[...]
 
-    left(u_send.at[0:240], 0)
+    left(u_turn.at[0:7], 0)
     left(e_send.at[0:240], 1)
-    left(u_turn.at[0:7], 2)
+    left(u_near.at[0:240], 2)
     left(m_one.at[0:15], 3)
     left(e_turn.at[0:7], 4)
     left(u_batch.at[0:3], 5)
     left(e_own.at[0:3], 7)
     left(m_two.at[0:7], 8)
-    left(g_send.at[0:254], 9)
+    left(g_send.at[0:240], 6)
+    left(g_turn.at[0:7], 9)
     left(m_three.at[0:3], 10)
 
 def grid_kernel(
@@ -455,7 +454,8 @@
         copy.start()
     stacked = []
     for g in range(4):
-        spectra = lanes([v_grid[64 * n : 64 * n + 64, 32 * g : 32 * g + 32] for n in range(4)])
+        received = v_grid[:, 32 * g : 32 * g + 32].reshape(8, 4, 8, 32)
+        spectra = lanes([received[:, n].reshape(64, 32) for n in range(4)])
         high, low = halves(spectra)
         along_x = dot(ix[...], jnp.concatenate([high, low, high], axis=0))
         stacked.append(lanes([along_x[:N], along_x[N:]]).astype(BF16))
@@ -481,7 +481,7 @@
     tables = [jnp.asarray(v) for v in make_tables()]
     exchange = [
         pltpu.VMEM((256, N), F32), pltpu.VMEM((256, N), F32),
-        pltpu.VMEM((8, 32, N), F32), pltpu.VMEM((8, 32, N), F32),
+        pltpu.VMEM((8, 32, N), F32), pltpu.VMEM((256, N), F32),
     ]
     anywhere = pl.BlockSpec(memory_space=pl.ANY)
     near = pl.BlockSpec(memory_space=pltpu.VMEM)
@@ -508,7 +508,8 @@
             pltpu.VMEM((2, 32, 32, N), BF16), pltpu.VMEM((32, 32), BF16),
             *(pltpu.VMEM(v.shape, BF16) for v in tables[:4]),
             pltpu.VMEM(field, BF16),
-            *exchange, *exchange, pltpu.VMEM((256, N), F32), pltpu.VMEM((256, N), F32),
+            *exchange, pltpu.VMEM((256, N), F32), pltpu.VMEM((256, N), F32), *exchange,
+            *exchange,
             pltpu.VMEM((64, N), F32), pltpu.VMEM((BATCH, 64, N), F32),
             pltpu.VMEM((4, 16, N), F32), pltpu.VMEM((BATCH, 16, N), F32),
             pltpu.VMEM((2, N, N), F32), pltpu.VMEM((2, 256, N), F32), pltpu.VMEM((2, N, N), F32),

time: 42.5 us -> 37.8 us (0.89)
  the two profiles are of different devices: /device:TPU:1 before, /device:TPU:4 now
where the time goes in v5:
time: 37.8 us; the launch traced here: 37.6 us
  Pallas kernels  37 us (98%)
  between operations  0.64 us (2%)
    pallas_call x1, Pallas kernels, on_device(): pl.pallas_call(spectral_kernel, out_shape=(jax.ShapeDtypeStruct((256, N),...  35.5 us
    pallas_call x1, Pallas kernels, on_device(): pl.pallas_call(grid_kernel, out_shape=(jax.ShapeDtypeStruct((4, 8, N, N),...  1.54 us

profile of v5, /device:TPU:4, one launch (start us, length us, event | category | flops | bytes accessed | tf_op | source)
XLA Modules:
  0.0 37.6 jit_solution(9130441829760211848)
XLA Ops:
  0.6 35.5 %shard_map.130 = (f32[256,128]{1,0:T(8,128)S(1)}, f32[32,128,128]{2,1,0:T(8,128)S(1)}, bf16[256,192]{1,0:T(8,128)(2,1)S(1)}, bf16[256,1024]{1,0:T(8,128)(2,1)S(1...) custom-call(bf16[32,128,128]{2,1,0:T(8,128)(2,1)} %bitcast.6, bf16[32,128,128]{2,1,0:T(8,128)(2,1)} %bitcast.7, ...), custom_call_target="tpu_custom_call" | custom-call | tf_op jit(solution)/shard_map/pallas_call | solution.py:494
  36.1 1.5 %shard_map.131 = (bf16[4,8,128,128]{3,2,1,0:T(8,128)(2,1)}, f32[2,32,8,128]{3,2,1,0:T(8,128)}, f32[32,32]{1,0:T(8,128)}) custom-call(f32[256,128]{1,0:T(8,128)S(1)} %get-tuple-element.12.v_grid, f32[32,128,128]{2,1,0:T(8,128)S(1)} %get-tuple-element.13.v_mix, bf16[256,192]{1,0:T(8,128)(2,1)S(1)} %get-tuple-element.14.ix, ...), custom_call_target="tpu_custom_call" | custom-call | tf_op jit(solution)/shard_map/pallas_call | solution.py:528

commit v6 on v5

--- a/solution.py
+++ b/solution.py
@@ -89,12 +89,11 @@
 
 
 def product(left, right, contracted):
-    def one(first, second):
-        return lax.dot_general(
-            first, second, ((contracted[:1], contracted[1:]), ((), ())), preferred_element_type=F32
-        )
-
-    return one(left[0], right[0]) + (one(left[1], right[0]) + one(left[0], right[1]))
+    first = jnp.concatenate([left[0], left[1], left[0]], axis=contracted[0])
+    second = jnp.concatenate([right[0], right[0], right[1]], axis=contracted[1])
+    return lax.dot_general(
+        first, second, ((contracted[:1], contracted[1:]), ((), ())), preferred_element_type=F32
+    )
 
 
 def lanes(blocks):
@@ -163,6 +162,17 @@
     prod, prod_rows, kron, skip_rows, m_own, m_one, m_two_own, m_two, m_three_own, m_three,
     load_sem, send_sem, recv_sem,
 ):
+    pairs = [
+        (pre_hbm, v_pre), (cot_hbm, v_cot), (fz_hbm, fz), (fx_hbm, fx), (in_hbm, v_in),
+        (skip_hbm, v_skip), (fy_hbm, fy), (weight_hbm, v_weight), (iy_hbm, iy), (ix_hbm, ix),
+        (iz_hbm, iz),
+    ]
+    loads = [
+        pltpu.make_async_copy(src, dst, load_sem.at[n]) for n, (src, dst) in enumerate(pairs)
+    ]
+    for copy in loads[:4]:
+        copy.start()
+
     sample = lax.axis_index("batch")
     place = lax.axis_index("space")
     a = place // 64
@@ -194,28 +204,14 @@
         return (sample + k) % BATCH
 
     barrier = pltpu.get_barrier_semaphore()
-    for _, where in [*near_first(), *far_first()]:
+    near_places, far_places = list(near_first()), far_first()
+    by_distance = near_places[:2] + far_places[:1] + near_places[2:6] + far_places[1:3]
+    for _, where in by_distance + near_places[6:] + far_places[3:]:
         pl.semaphore_signal(barrier, inc=1, device_id={"space": where}, device_id_type=MESH)
 
     @pl.loop(1, BATCH)
     def _(k):
         pl.semaphore_signal(barrier, inc=1, device_id={"batch": other(k)}, device_id_type=MESH)
-
-    def group(ref, g):
-        return ref.at[8 * g : 8 * g + 8]
-
-    pairs = []
-    for g in range(4):
-        pairs += [(group(src, g), group(dst, g)) for src, dst in ((pre_hbm, v_pre), (cot_hbm, v_cot))]
-    pairs += [
-        (fz_hbm, fz), (fx_hbm, fx), (in_hbm, v_in), (skip_hbm, v_skip), (fy_hbm, fy), (weight_hbm, v_weight),
-        (iy_hbm, iy), (ix_hbm, ix), (iz_hbm, iz),
-    ]
-    loads = [
-        pltpu.make_async_copy(src, dst, load_sem.at[n]) for n, (src, dst) in enumerate(pairs)
-    ]
-    for copy in loads[:10]:
-        copy.start()
 
     def remote(src, dst, n, where):
         return pltpu.make_async_remote_copy(
@@ -250,22 +246,23 @@
     def left(ref, n):
         pltpu.make_async_copy(ref, ref, send_sem.at[n]).wait()
 
+    loads[4].start()
+    loads[0].wait()
+    loads[1].wait()
     for g in range(4):
-        loads[2 * g].wait()
-        loads[2 * g + 1].wait()
         for c in range(8 * g, 8 * g + 8):
             slope = gelu_slope(v_pre[c].astype(F32))
             v_cp[c] = (v_cot[c].astype(F32) * slope).astype(BF16)
-    for copy in loads[10:]:
-        copy.start()
-    loads[8].wait()
-    loads[9].wait()
+    loads[2].wait()
+    loads[3].wait()
     sections = all_sections(v_cp, fz, fx)
     to_blocks(sections, e_send)
     pl.semaphore_wait(barrier, 15 + 7 + BATCH - 1)
     send_near(e_send, e_mid, 1)
-
-    loads[10].wait()
+    for copy in loads[5:]:
+        copy.start()
+
+    loads[4].wait()
     to_blocks(all_sections(v_in, fz, fx), u_send)
     turn(u_send, u_turn)
     send_far(u_turn, u_mid, 0)
@@ -312,7 +309,7 @@
     cross(u_mid, u_near)
     send_near(u_near, u_last, 2)
 
-    loads[11].wait()
+    loads[5].wait()
     tall = lax.broadcasted_iota(jnp.int32, (32, 512), 1) // 16
     spread_t = tall == lax.broadcasted_iota(jnp.int32, (32, 512), 0)
     repeated = dot(v_skip[...], spread_t.astype(F32).astype(BF16))
@@ -341,7 +338,7 @@
         remote(m_two_own, m_two.at[b], 8, {"space": far(k)[1]}).start()
 
     arrived(e_all, 4)
-    loads[12].wait()
+    loads[6].wait()
     e_rounded = []
 
     def put_e(part, value):
@@ -351,7 +348,7 @@
 
     along_y(e_all, fy, rows, put_e)
 
-    loads[13].wait()
+    loads[7].wait()
     e_real, e_imag = e_rounded
     for i in range(CHANNELS):
         w_real = v_weight[0, i].astype(F32)
@@ -373,7 +370,7 @@
         value = value * scale
         for k4 in range(4):
             back_rows[part, pl.ds(k4, 32, stride=4), :] = jnp.where(block == k4, value, 0.0)
-    loads[14].wait()
+    loads[8].wait()
     back = halves(lanes([back_rows[0], back_rows[1]]))
     g_send[...] = product((iy[0], iy[1]), back, (1, 1))
     send_near(g_send, g_mid, 6)
@@ -426,8 +423,8 @@
     for r in range(4):
         v_mixgrad[8 * r : 8 * r + 8, :] = total[:, 32 * r : 32 * r + 32]
 
-    loads[15].wait()
-    loads[16].wait()
+    loads[9].wait()
+    loads[10].wait()
     arrived(g_all, 9)
     v_grid[...] = g_all[...]
 
@@ -518,7 +515,7 @@
             pltpu.VMEM((8, N), F32), pltpu.VMEM((16, 8, N), F32),
             pltpu.VMEM((8, N), F32), pltpu.VMEM((8, 8, N), F32),
             pltpu.VMEM((8, N), F32), pltpu.VMEM((BATCH, 8, N), F32),
-            pltpu.SemaphoreType.DMA((17,)),
+            pltpu.SemaphoreType.DMA((11,)),
             pltpu.SemaphoreType.DMA((11,)), pltpu.SemaphoreType.DMA((11,)),
         ],
         compiler_params=pltpu.CompilerParams(

time: 37.8 us -> 37.8 us (level)
  the two profiles are of different devices: /device:TPU:4 before, /device:TPU:8 now
where the time goes in v6:
time: 37.8 us; the launch traced here: 37.7 us
  Pallas kernels  37 us (98%)
  between operations  0.64 us (2%)
    pallas_call x1, Pallas kernels, on_device(): pl.pallas_call(spectral_kernel, out_shape=(jax.ShapeDtypeStruct((256, N),...  35.5 us
    pallas_call x1, Pallas kernels, on_device(): pl.pallas_call(grid_kernel, out_shape=(jax.ShapeDtypeStruct((4, 8, N, N),...  1.56 us

profile of v6, /device:TPU:8, one launch (start us, length us, event | category | flops | bytes accessed | tf_op | source)
XLA Modules:
  0.0 37.7 jit_solution(5581514452767188465)
XLA Ops:
  0.6 35.5 %shard_map.130 = (f32[256,128]{1,0:T(8,128)S(1)}, f32[32,128,128]{2,1,0:T(8,128)S(1)}, bf16[256,192]{1,0:T(8,128)(2,1)S(1)}, bf16[256,1024]{1,0:T(8,128)(2,1)S(1...) custom-call(bf16[32,128,128]{2,1,0:T(8,128)(2,1)} %bitcast.6, bf16[32,128,128]{2,1,0:T(8,128)(2,1)} %bitcast.7, ...), custom_call_target="tpu_custom_call" | custom-call | tf_op jit(solution)/shard_map/pallas_call | solution.py:491
  36.1 1.6 %shard_map.131 = (bf16[4,8,128,128]{3,2,1,0:T(8,128)(2,1)}, f32[2,32,8,128]{3,2,1,0:T(8,128)}, f32[32,32]{1,0:T(8,128)}) custom-call(f32[256,128]{1,0:T(8,128)S(1)} %get-tuple-element.12.v_grid, f32[32,128,128]{2,1,0:T(8,128)S(1)} %get-tuple-element.13.v_mix, bf16[256,192]{1,0:T(8,128)(2,1)S(1)} %get-tuple-element.14.ix, ...), custom_call_target="tpu_custom_call" | custom-call | tf_op jit(solution)/shard_map/pallas_call | solution.py:525
